TPU v7x, 32 devices: a whole 2x2x4 slice. The times are simulated.
32 devices in a mesh: dp: 2 (over core), narrow: 4 (over y, x), wide: 4 (over z).
Axes of the slice: x: 2, y: 2, z: 4, core: 2. Of those that a mesh axis runs over, the one named last changes fastest.
Arguments:
- tokens: bfloat16 [8192, 2048], P(('dp', 'narrow', 'wide')), may hold values from -6 to 6
- document_lengths: int32 [8, 8], P(('dp', 'narrow')), may hold values from 1 to 512, 1024 in all within a row
- attn_gain: bfloat16 [2048], P('narrow'), may hold values from 0.5 to 1.5
- query_projection_weight: bfloat16 [2048, 2048], P('narrow', 'wide'), may hold values from -0.125 to 0.125
- key_projection_weight: bfloat16 [2048, 512], P('narrow'), may hold values from -0.125 to 0.125
- value_projection_weight: bfloat16 [2048, 512], P('narrow'), may hold values from -0.125 to 0.125
- output_weight: bfloat16 [2048, 2048], P('wide', 'narrow'), may hold values from -1 to 1
- mlp_gain: bfloat16 [2048], P('narrow'), may hold values from 0.5 to 1.5
- gate_weight: bfloat16 [2048, 8192], P('narrow', 'wide'), may hold values from -0.125 to 0.125
- up_weight: bfloat16 [2048, 8192], P('narrow', 'wide'), may hold values from -0.125 to 0.125
- down_weight: bfloat16 [8192, 2048], P('wide', 'narrow'), may hold values from -0.0625 to 0.0625
- output_cotangent: bfloat16 [8192, 2048], P(('dp', 'narrow', 'wide')), may hold values from -6 to 6
Outputs:
- layer_out: bfloat16 [8192, 2048], P(('dp', 'narrow', 'wide'))
- tokens_grad: float32 [8192, 2048], P(('dp', 'narrow', 'wide'))
- attn_gain_grad: float32 [2048], P(('dp', 'narrow', 'wide'))
- query_grad: float32 [2048, 2048], P(('dp', 'narrow'), 'wide')
- key_grad: float32 [2048, 512], P(('dp', 'narrow'), 'wide')
- value_grad: float32 [2048, 512], P(('dp', 'narrow'), 'wide')
- output_grad: float32 [2048, 2048], P('wide', ('dp', 'narrow'))
- mlp_gain_grad: float32 [2048], P(('dp', 'narrow', 'wide'))
- gate_grad: float32 [2048, 8192], P(('dp', 'narrow'), 'wide')
- up_grad: float32 [2048, 8192], P(('dp', 'narrow'), 'wide')
- down_grad: float32 [8192, 2048], P('wide', ('dp', 'narrow'))
Inputs may be any that keep to these rules, and one draw needn't show every extreme that they name: `document_lengths`: in every row the 8 lengths are 1 or more and sum to 1024, and the longest is exactly 512.
All inputs are finite; a program needn't handle non-finite values.
Results may differ from a plain program's by a relative error of at most 0.025.
Values may be sent and summed in bfloat16 or wider, within the bound.
No kernel may reach another device: no remote copies, remote signals or barrier semaphores. Data moves between devices by JAX's collectives and lax.ppermute only.
A program may use at most 320 MiB of HBM per device.

v0:
```python
import math

import jax
import jax.numpy as jnp
from jax import lax
from jax.sharding import PartitionSpec as P

QUERY_HEADS = 32
KEY_VALUE_HEADS = 8
HEAD_SIZE = 64


epsilon = 1e-05
masked_score = -1e30


def rope_tables(positions, head_dim):
    half_dim = head_dim // 2
    freq_index = jnp.arange(half_dim, dtype=jnp.float32)
    inverse = 500000.0 ** (-2.0 * freq_index / head_dim)
    wavelength = 2.0 * math.pi / inverse
    smooth_part = (8192.0 / wavelength - 1.0) / 3.0
    blended = (1.0 - smooth_part) * inverse / 32.0 + smooth_part * inverse
    scaled = jnp.where(
        wavelength < 2048.0, inverse, jnp.where(wavelength > 8192.0, inverse / 32.0, blended)
    )
    angles = positions.astype(jnp.float32)[:, None] * scaled[None, :]
    cosine = jnp.cos(angles)
    sine_table = jnp.sin(angles)
    return (jnp.concatenate([cosine, cosine], 1), jnp.concatenate([sine_table, sine_table], 1))


def rotate(value_rows_matrix, cosine, sine_table):
    half_dim = value_rows_matrix.shape[-1] // 2
    turned = jnp.concatenate(
        [-value_rows_matrix[..., half_dim:], value_rows_matrix[..., :half_dim]], -1
    )
    return value_rows_matrix * cosine[:, None, :] + turned * sine_table[:, None, :]


def rotate_back(grads, cosine, sine_table):
    half_dim = grads.shape[-1] // 2
    scaled = grads * sine_table[:, None, :]
    turned = jnp.concatenate([scaled[..., half_dim:], -scaled[..., :half_dim]], -1)
    return grads * cosine[:, None, :] + turned


def row_layout(row_lengths, row_length):
    ends = jnp.cumsum(row_lengths)
    starts = ends - row_lengths
    token_positions_list = jnp.arange(row_length, dtype=jnp.int32)
    segment = jnp.sum((token_positions_list[:, None] >= ends[None, :]).astype(jnp.int32), 1)
    chosen = segment[:, None] == jnp.arange(row_lengths.shape[0], dtype=jnp.int32)[None, :]
    position = token_positions_list - jnp.sum(jnp.where(chosen, starts[None, :], 0), 1)
    return (segment, position)


def block_scores(
    query_part,
    query_segment,
    query_places,
    key_row_matrix,
    segment,
    token_positions_list,
    key_first,
    row_block_list,
):
    key_part = lax.dynamic_slice_in_dim(key_row_matrix, key_first, row_block_list, 0)
    key_segment = lax.dynamic_slice_in_dim(segment, key_first, row_block_list, 0)
    key_places = lax.dynamic_slice_in_dim(token_positions_list, key_first, row_block_list, 0)
    scores = jnp.einsum(
        "qhd,khd->hqk", query_part, key_part, preferred_element_type=jnp.float32
    ) * (1.0 / math.sqrt(query_part.shape[-1]))
    visible = (query_segment[:, None] == key_segment[None, :]) & (
        query_places[:, None] >= key_places[None, :]
    )
    return (jnp.where(visible[None], scores, masked_score), key_part)


def block_live(segment, query_index, key_index, row_block_list):
    return (key_index <= query_index) & (
        segment[key_index * row_block_list + row_block_list - 1]
        >= segment[query_index * row_block_list]
    )


def keep_state(current):
    return current


def rows_of_wide(rows):
    return lax.all_gather(rows, "wide", axis=0, tiled=True)


def attention_forward(
    query_rows_matrix, key_row_matrix, value_rows_matrix, segment, row_block_list
):
    length, head_count, head_dim = query_rows_matrix.shape
    block_list = length // row_block_list
    token_positions_list = jnp.arange(length, dtype=jnp.int32)

    def query_block(query_index):
        query_first = query_index * row_block_list
        query_part = lax.dynamic_slice_in_dim(query_rows_matrix, query_first, row_block_list, 0)
        query_segment = lax.dynamic_slice_in_dim(segment, query_first, row_block_list, 0)
        query_places = lax.dynamic_slice_in_dim(
            token_positions_list, query_first, row_block_list, 0
        )

        def total_step(key_index, carried):

            def total_visit(current):
                running, summed = current
                scores, ignored = block_scores(
                    query_part,
                    query_segment,
                    query_places,
                    key_row_matrix,
                    segment,
                    token_positions_list,
                    key_index * row_block_list,
                    row_block_list,
                )
                largest = jnp.maximum(running, jnp.max(scores, -1))
                summed = summed * jnp.exp(running - largest) + jnp.sum(
                    jnp.exp(scores - largest[..., None]), -1
                )
                return (largest, summed)

            return lax.cond(
                block_live(segment, query_index, key_index, row_block_list),
                total_visit,
                keep_state,
                carried,
            )

        start_state = (
            jnp.full((head_count, row_block_list), masked_score, jnp.float32),
            jnp.zeros((head_count, row_block_list), jnp.float32),
        )
        running, summed = lax.fori_loop(0, block_list, total_step, start_state)
        log_total = running + jnp.log(summed)

        def value_step(key_index, output):

            def value_visit(current):
                scores, ignored = block_scores(
                    query_part,
                    query_segment,
                    query_places,
                    key_row_matrix,
                    segment,
                    token_positions_list,
                    key_index * row_block_list,
                    row_block_list,
                )
                weights_low = jnp.exp(scores - log_total[..., None]).astype(jnp.bfloat16)
                value_part = lax.dynamic_slice_in_dim(
                    value_rows_matrix, key_index * row_block_list, row_block_list, 0
                )
                return current + jnp.einsum(
                    "hqk,khd->qhd", weights_low, value_part, preferred_element_type=jnp.float32
                )

            return lax.cond(
                block_live(segment, query_index, key_index, row_block_list),
                value_visit,
                keep_state,
                output,
            )

        attended = lax.fori_loop(
            0,
            block_list,
            value_step,
            jnp.zeros((row_block_list, head_count, head_dim), jnp.float32),
        )
        return (attended, log_total)

    attended, log_totals = lax.map(query_block, jnp.arange(block_list, dtype=jnp.int32))
    return (attended.reshape(length, head_count, head_dim), log_totals)


def attention_backward(
    query_rows_matrix,
    key_row_matrix,
    value_rows_matrix,
    attended_grad,
    row_dots,
    log_totals,
    segment,
    row_block_list,
):
    length, head_count, head_dim = query_rows_matrix.shape
    block_list = length // row_block_list
    token_positions_list = jnp.arange(length, dtype=jnp.int32)
    score_scale = 1.0 / math.sqrt(head_dim)

    def query_block(carried, query_index):
        query_first = query_index * row_block_list
        query_part = lax.dynamic_slice_in_dim(query_rows_matrix, query_first, row_block_list, 0)
        query_segment = lax.dynamic_slice_in_dim(segment, query_first, row_block_list, 0)
        query_places = lax.dynamic_slice_in_dim(
            token_positions_list, query_first, row_block_list, 0
        )
        grad_part = lax.dynamic_slice_in_dim(attended_grad, query_first, row_block_list, 0)
        dot_part = lax.dynamic_slice_in_dim(row_dots, query_first, row_block_list, 1)
        total_part = log_totals[query_index]

        def key_step(key_index, inner):

            def key_visit(current):
                query_grad, key_grads, value_grads = current
                key_first = key_index * row_block_list
                scores, key_part = block_scores(
                    query_part,
                    query_segment,
                    query_places,
                    key_row_matrix,
                    segment,
                    token_positions_list,
                    key_first,
                    row_block_list,
                )
                weights = jnp.exp(scores - total_part[..., None])
                value_part = lax.dynamic_slice_in_dim(
                    value_rows_matrix, key_first, row_block_list, 0
                )
                weight_grads = jnp.einsum(
                    "qhd,khd->hqk", grad_part, value_part, preferred_element_type=jnp.float32
                )
                score_low = (weights * (weight_grads - dot_part[..., None])).astype(jnp.bfloat16)
                query_grad = (
                    query_grad
                    + jnp.einsum(
                        "hqk,khd->qhd", score_low, key_part, preferred_element_type=jnp.float32
                    )
                    * score_scale
                )
                key_add = (
                    jnp.einsum(
                        "hqk,qhd->khd", score_low, query_part, preferred_element_type=jnp.float32
                    )
                    * score_scale
                )
                value_add = jnp.einsum(
                    "hqk,qhd->khd",
                    weights.astype(jnp.bfloat16),
                    grad_part,
                    preferred_element_type=jnp.float32,
                )
                key_grads = lax.dynamic_update_slice_in_dim(
                    key_grads,
                    lax.dynamic_slice_in_dim(key_grads, key_first, row_block_list, 0) + key_add,
                    key_first,
                    0,
                )
                value_grads = lax.dynamic_update_slice_in_dim(
                    value_grads,
                    lax.dynamic_slice_in_dim(value_grads, key_first, row_block_list, 0) + value_add,
                    key_first,
                    0,
                )
                return (query_grad, key_grads, value_grads)

            return lax.cond(
                block_live(segment, query_index, key_index, row_block_list),
                key_visit,
                keep_state,
                inner,
            )

        zero_block = jnp.zeros((row_block_list, head_count, head_dim), jnp.float32)
        query_grad, key_grads, value_grads = lax.fori_loop(
            0, block_list, key_step, (zero_block, carried[0], carried[1])
        )
        return ((key_grads, value_grads), query_grad)

    empty_grads = jnp.zeros((length, head_count, head_dim), jnp.float32)
    (key_grads, value_grads), query_grads = lax.scan(
        query_block, (empty_grads, empty_grads), jnp.arange(block_list, dtype=jnp.int32)
    )
    return (query_grads.reshape(length, head_count, head_dim), key_grads, value_grads)


def on_device(
    tokens,
    document_lengths,
    attn_gain,
    query_projection_weight,
    key_projection_weight,
    value_projection_weight,
    output_weight,
    mlp_gain,
    gate_weight,
    up_weight,
    down_weight,
    output_cotangent,
):
    wide_count = lax.axis_size("wide")
    wide_index = lax.axis_index("wide")
    outer_count = lax.axis_size("dp") * lax.axis_size("narrow")
    head_dim = HEAD_SIZE
    local_heads = query_projection_weight.shape[1] // head_dim
    group_size = QUERY_HEADS // KEY_VALUE_HEADS
    local_kv = max(1, local_heads // group_size)
    repeat_count = local_heads // local_kv
    kv_first = wide_index * local_heads // group_size
    query_count = local_heads * head_dim
    kv_count = local_kv * head_dim
    own_rows = tokens.shape[0]
    row_length = own_rows * wide_count
    row_block_list = min(512, row_length)
    key_own = lax.dynamic_slice_in_dim(key_projection_weight, kv_first * head_dim, kv_count, 1)
    value_own = lax.dynamic_slice_in_dim(value_projection_weight, kv_first * head_dim, kv_count, 1)
    (
        query_full,
        key_full,
        value_full,
        gate_full,
        up_full,
        attn_gain_full,
        mlp_gain_full,
        output_narrow,
        down_full,
    ) = (
        lax.all_gather(query_projection_weight, "narrow", axis=0, tiled=True),
        lax.all_gather(key_own, "narrow", axis=0, tiled=True),
        lax.all_gather(value_own, "narrow", axis=0, tiled=True),
        lax.all_gather(gate_weight, "narrow", axis=0, tiled=True),
        lax.all_gather(up_weight, "narrow", axis=0, tiled=True),
        lax.all_gather(attn_gain, "narrow", axis=0, tiled=True),
        lax.all_gather(mlp_gain, "narrow", axis=0, tiled=True),
        lax.all_gather(output_weight, "narrow", axis=1, tiled=True),
        lax.all_gather(down_weight, "narrow", axis=1, tiled=True),
    )
    project_weight = jnp.concatenate([query_full, key_full, value_full], 1)
    inputs = tokens.astype(jnp.float32)
    inv_first = lax.rsqrt(jnp.mean(inputs * inputs, -1, keepdims=True) + epsilon)
    unit_first = inputs * inv_first
    normed_input = (unit_first * attn_gain_full.astype(jnp.float32)).astype(jnp.bfloat16)
    normed_all = rows_of_wide(normed_input)
    projected = jnp.dot(normed_all, project_weight, preferred_element_type=jnp.float32)
    segment, position = row_layout(document_lengths[0], row_length)
    cosine, sine_table = rope_tables(position, head_dim)
    query_rows_matrix = rotate(
        projected[:, :query_count].reshape(row_length, local_heads, head_dim), cosine, sine_table
    ).astype(jnp.bfloat16)
    key_row_matrix = rotate(
        projected[:, query_count : query_count + kv_count].reshape(row_length, local_kv, head_dim),
        cosine,
        sine_table,
    ).astype(jnp.bfloat16)
    value_rows_matrix = (
        projected[:, query_count + kv_count :]
        .astype(jnp.bfloat16)
        .reshape(row_length, local_kv, head_dim)
    )
    keys_wide = jnp.repeat(key_row_matrix, repeat_count, axis=1)
    values_wide = jnp.repeat(value_rows_matrix, repeat_count, axis=1)
    attended, log_totals = attention_forward(
        query_rows_matrix, keys_wide, values_wide, segment, row_block_list
    )
    attended = attended.reshape(row_length, query_count)
    attended_low = attended.astype(jnp.bfloat16)
    branch = lax.psum_scatter(
        jnp.dot(attended_low, output_narrow, preferred_element_type=jnp.float32).astype(
            jnp.bfloat16
        ),
        "wide",
        scatter_dimension=0,
        tiled=True,
    ).astype(jnp.float32)
    hidden = inputs + branch
    inv_second = lax.rsqrt(jnp.mean(hidden * hidden, -1, keepdims=True) + epsilon)
    unit_second = hidden * inv_second
    normed_mlp = (unit_second * mlp_gain_full.astype(jnp.float32)).astype(jnp.bfloat16)
    normed_mlp_all = rows_of_wide(normed_mlp)
    gate_value = jnp.dot(normed_mlp_all, gate_full, preferred_element_type=jnp.float32)
    up_value = jnp.dot(normed_mlp_all, up_full, preferred_element_type=jnp.float32)
    sigmoid_gate = jax.nn.sigmoid(gate_value)
    silu_gate = gate_value * sigmoid_gate
    activated = (silu_gate * up_value).astype(jnp.bfloat16)
    mlp_branch = lax.psum_scatter(
        jnp.dot(activated, down_full, preferred_element_type=jnp.float32).astype(jnp.bfloat16),
        "wide",
        scatter_dimension=0,
        tiled=True,
    ).astype(jnp.float32)
    layer_out = (hidden + mlp_branch).astype(jnp.bfloat16)
    upstream = output_cotangent.astype(jnp.float32)
    upstream_all = rows_of_wide(output_cotangent)
    act_grad = jnp.einsum("td,fd->tf", upstream_all, down_full, preferred_element_type=jnp.float32)
    down_grad = jnp.einsum("tf,td->fd", activated, upstream_all, preferred_element_type=jnp.float32)
    gate_low = (
        act_grad * up_value * (sigmoid_gate * (1.0 + gate_value * (1.0 - sigmoid_gate)))
    ).astype(jnp.bfloat16)
    up_low = (act_grad * silu_gate).astype(jnp.bfloat16)
    gate_grad = jnp.einsum(
        "td,tf->df", normed_mlp_all, gate_low, preferred_element_type=jnp.float32
    )
    up_grad = jnp.einsum("td,tf->df", normed_mlp_all, up_low, preferred_element_type=jnp.float32)
    normed_mlp_grad = lax.psum_scatter(
        (
            jnp.einsum("tf,df->td", gate_low, gate_full, preferred_element_type=jnp.float32)
            + jnp.einsum("tf,df->td", up_low, up_full, preferred_element_type=jnp.float32)
        ).astype(jnp.bfloat16),
        "wide",
        scatter_dimension=0,
        tiled=True,
    ).astype(jnp.float32)
    scaled_second = normed_mlp_grad * mlp_gain_full.astype(jnp.float32)
    mlp_gain_part = jnp.sum(normed_mlp_grad * unit_second, 0)
    hidden_grad = upstream + inv_second * (
        scaled_second - unit_second * jnp.mean(scaled_second * unit_second, -1, keepdims=True)
    )
    hidden_low = hidden_grad.astype(jnp.bfloat16)
    hidden_all = lax.all_gather(hidden_low, "wide", axis=0, tiled=True)
    attended_grad = jnp.einsum(
        "td,hd->th", hidden_all, output_narrow, preferred_element_type=jnp.float32
    ).astype(jnp.bfloat16)
    output_grad = jnp.einsum(
        "th,td->hd", attended_low, hidden_all, preferred_element_type=jnp.float32
    )
    row_dots = jnp.sum(
        (attended_grad.astype(jnp.float32) * attended).reshape(row_length, local_heads, head_dim),
        -1,
    ).T
    query_grads, key_grads, value_grads = attention_backward(
        query_rows_matrix,
        keys_wide,
        values_wide,
        attended_grad.reshape(row_length, local_heads, head_dim),
        row_dots,
        log_totals,
        segment,
        row_block_list,
    )
    key_grads = key_grads.reshape(row_length, local_kv, repeat_count, head_dim).sum(2)
    value_grads = value_grads.reshape(row_length, local_kv, repeat_count, head_dim).sum(2)
    query_low = (
        rotate_back(query_grads, cosine, sine_table)
        .astype(jnp.bfloat16)
        .reshape(row_length, query_count)
    )
    key_low = (
        rotate_back(key_grads, cosine, sine_table)
        .astype(jnp.bfloat16)
        .reshape(row_length, kv_count)
    )
    value_low = value_grads.astype(jnp.bfloat16).reshape(row_length, kv_count)
    projected_low = jnp.concatenate([query_low, key_low, value_low], 1)
    project_grad = jnp.einsum(
        "td,tc->dc", normed_all, projected_low, preferred_element_type=jnp.float32
    )
    normed_grad = lax.psum_scatter(
        jnp.einsum(
            "tc,dc->td", projected_low, project_weight, preferred_element_type=jnp.float32
        ).astype(jnp.bfloat16),
        "wide",
        scatter_dimension=0,
        tiled=True,
    ).astype(jnp.float32)
    scaled_first = normed_grad * attn_gain_full.astype(jnp.float32)
    attn_gain_part = jnp.sum(normed_grad * unit_first, 0)
    tokens_grad = hidden_grad + inv_first * (
        scaled_first - unit_first * jnp.mean(scaled_first * unit_first, -1, keepdims=True)
    )
    model_rows = project_grad.shape[0]
    total_kv = key_projection_weight.shape[1]
    key_embed = lax.dynamic_update_slice_in_dim(
        jnp.zeros((model_rows, total_kv), jnp.float32),
        project_grad[:, query_count : query_count + kv_count],
        kv_first * head_dim,
        1,
    )
    value_embed = lax.dynamic_update_slice_in_dim(
        jnp.zeros((model_rows, total_kv), jnp.float32),
        project_grad[:, query_count + kv_count :],
        kv_first * head_dim,
        1,
    )

    def reorder(gain_part):
        return gain_part.reshape(outer_count, wide_count, -1).transpose(1, 0, 2).reshape(-1)

    key_part, value_part, attn_gain_wide, mlp_gain_wide = (
        lax.psum_scatter(
            key_embed.astype(jnp.bfloat16), "wide", scatter_dimension=1, tiled=True
        ).astype(jnp.float32),
        lax.psum_scatter(
            value_embed.astype(jnp.bfloat16), "wide", scatter_dimension=1, tiled=True
        ).astype(jnp.float32),
        lax.psum_scatter(
            reorder(attn_gain_part).astype(jnp.bfloat16), "wide", scatter_dimension=0, tiled=True
        ).astype(jnp.float32),
        lax.psum_scatter(
            reorder(mlp_gain_part).astype(jnp.bfloat16), "wide", scatter_dimension=0, tiled=True
        ).astype(jnp.float32),
    )
    (
        query_grad,
        key_grad,
        value_grad,
        gate_grad,
        up_grad,
        attn_gain_grad,
        mlp_gain_grad,
        output_grad,
        down_grad,
    ) = (
        lax.psum_scatter(
            project_grad[:, :query_count].astype(jnp.bfloat16),
            ("dp", "narrow"),
            scatter_dimension=0,
            tiled=True,
        ).astype(jnp.float32),
        lax.psum_scatter(
            key_part.astype(jnp.bfloat16), ("dp", "narrow"), scatter_dimension=0, tiled=True
        ).astype(jnp.float32),
        lax.psum_scatter(
            value_part.astype(jnp.bfloat16), ("dp", "narrow"), scatter_dimension=0, tiled=True
        ).astype(jnp.float32),
        lax.psum_scatter(
            gate_grad.astype(jnp.bfloat16), ("dp", "narrow"), scatter_dimension=0, tiled=True
        ).astype(jnp.float32),
        lax.psum_scatter(
            up_grad.astype(jnp.bfloat16), ("dp", "narrow"), scatter_dimension=0, tiled=True
        ).astype(jnp.float32),
        lax.psum_scatter(
            attn_gain_wide.astype(jnp.bfloat16), ("dp", "narrow"), scatter_dimension=0, tiled=True
        ).astype(jnp.float32),
        lax.psum_scatter(
            mlp_gain_wide.astype(jnp.bfloat16), ("dp", "narrow"), scatter_dimension=0, tiled=True
        ).astype(jnp.float32),
        lax.psum_scatter(
            output_grad.astype(jnp.bfloat16), ("dp", "narrow"), scatter_dimension=1, tiled=True
        ).astype(jnp.float32),
        lax.psum_scatter(
            down_grad.astype(jnp.bfloat16), ("dp", "narrow"), scatter_dimension=1, tiled=True
        ).astype(jnp.float32),
    )
    return (
        layer_out,
        tokens_grad,
        attn_gain_grad,
        query_grad,
        key_grad,
        value_grad,
        output_grad,
        mlp_gain_grad,
        gate_grad,
        up_grad,
        down_grad,
    )


def solution(mesh):
    return jax.shard_map(
        on_device,
        mesh=mesh,
        in_specs=(
            P(("dp", "narrow", "wide"), None),
            P(("dp", "narrow"), None),
            P("narrow"),
            P("narrow", "wide"),
            P("narrow", None),
            P("narrow", None),
            P("wide", "narrow"),
            P("narrow"),
            P("narrow", "wide"),
            P("narrow", "wide"),
            P("wide", "narrow"),
            P(("dp", "narrow", "wide"), None),
        ),
        out_specs=(
            P(("dp", "narrow", "wide"), None),
            P(("dp", "narrow", "wide"), None),
            P(("dp", "narrow", "wide")),
            P(("dp", "narrow"), "wide"),
            P(("dp", "narrow"), "wide"),
            P(("dp", "narrow"), "wide"),
            P("wide", ("dp", "narrow")),
            P(("dp", "narrow", "wide")),
            P(("dp", "narrow"), "wide"),
            P(("dp", "narrow"), "wide"),
            P("wide", ("dp", "narrow")),
        ),
        check_vma=False,
    )
```

profile of v0, /device:TPU:8, one launch (start us, length us, event | category | flops | bytes accessed | tf_op | source)
XLA Modules:
  0.0 1761.7 jit_solution(11129403382742146986)
XLA Ops:
  8.7 8.1 all-gather
  22.4 11.1 all_gather.42
  34.7 13.4 all_gather.43
  50.9 3.1 constant_dynamic-update-slice_fusion.2
  55.8 75.4 %all-gather.12.cloned.1.call-done = bf16[1024,2048]{1,0:T(8,128)(2,1)} async-done(((bf16[256,2048]{1,0:T(8,128)(2,1)}), bf16[1024,2048]{1,0:T(8,128)(2,1)}) %all-gather.12.cloned.1.call-update) | async-done | bytes 4194320 | tf_op jit(solution)/shard_map/all_gather | solution.py:92
  131.2 6.6 fusion.98
  142.0 97.4 %while.154 = (s32[]{:T(128)}, f32[2,512,8,64]{1,0,3,2:T(2,128)}, f32[2,8,512]{2,1,0:T(8,128)S(1)}, s32[2]{0:T(128)S(1)}, bf16[1024,8,64]{0,2,1:T(8,128)(2,1)}, /...) while((s32[]{:T(128)}, f32[2,512,8,64]{1,0,3,2:T(2,128)}, ...), condition=%wide.region_15.16_spmd.clone.clone, body=%wide.region_4.15_spmd.clone.clone.sunk | while | flops 830222336 | bytes 32090500 | solution.py:180
  145.2 8.9 while.157
  147.8 3.7 conditional.7
  155.3 9.5 while.158
  157.9 4.4 conditional.8
  158.4 3.9 fusion.23
  165.9 19.6 %dynamic_update_slice.58 = f32[2,512,8,64]{1,0,3,2:T(2,128)} dynamic-update-slice(f32[2,512,8,64]{1,0,3,2:T(2,128)} %get-tuple-element.2962, f32[1,512,8,64]{1,0,3,2:T(1,128)S(1)} %copy.93, s32[]{:T(128)} %get-tuple-element.2961, s32[]{:T(128)} %constant.395.clone.1..sunk, s32[]{:T(128)} %constant.395.clone.1..sunk, s32[]{:T(128)} %constant.395.clone.1..sunk) | dynamic-update-slice | bytes 2097156 | tf_op jit(solution)/shard_map/while/body/jit(dynamic_update_index_in_dim)/dynamic_update_slice | solution.py:180
  188.8 8.9 while.157
  193.9 3.7 conditional.7
  198.9 9.5 while.158
  204.0 4.4 conditional.8
  204.5 3.9 fusion.23
  209.5 19.6 %dynamic_update_slice.58 = f32[2,512,8,64]{1,0,3,2:T(2,128)} dynamic-update-slice(f32[2,512,8,64]{1,0,3,2:T(2,128)} %get-tuple-element.2962, f32[1,512,8,64]{1,0,3,2:T(1,128)S(1)} %copy.93, s32[]{:T(128)} %get-tuple-element.2961, s32[]{:T(128)} %constant.395.clone.1..sunk, s32[]{:T(128)} %constant.395.clone.1..sunk, s32[]{:T(128)} %constant.395.clone.1..sunk) | dynamic-update-slice | bytes 2097156 | tf_op jit(solution)/shard_map/while/body/jit(dynamic_update_index_in_dim)/dynamic_update_slice | solution.py:180
  241.5 6.7 convolution_convert_fusion.4
  248.9 16.3 all-gather.1
  265.2 69.2 %reduce-scatter.18.cloned.1.call-done = bf16[256,2048]{1,0:T(8,128)(2,1)} async-done(((bf16[1024,2048]{1,0:T(8,128)(2,1)}), bf16[256,2048]{1,0:T(8,128)(2,1)}) %reduce-scatter.18.cloned.1.call-update) | async-done | bytes 1048592 | tf_op jit(solution)/shard_map/reduce_scatter | solution.py:366
  341.0 83.4 %all-gather.22.cloned.1.call-done = bf16[2048,2048]{1,0:T(8,128)(2,1)} async-done(((bf16[512,2048]{1,0:T(8,128)(2,1)}), bf16[2048,2048]{1,0:T(8,128)(2,1)}) %all-gather.22.cloned.1.call-update) | async-done | bytes 8388624 | tf_op jit(solution)/shard_map/all_gather | solution.py:331
  424.4 80.2 %all-gather.18.cloned.1.call-done = bf16[1024,2048]{1,0:T(8,128)(2,1)} async-done(((bf16[256,2048]{1,0:T(8,128)(2,1)}), bf16[1024,2048]{1,0:T(8,128)(2,1)}) %all-gather.18.cloned.1.call-update) | async-done | bytes 4194320 | tf_op jit(solution)/shard_map/all_gather | solution.py:92
  504.6 14.6 fusion.100
  519.2 76.2 %all-gather.20.cloned.1.call-done = bf16[2048,2048]{1,0:T(8,128)(2,1)} async-done(((bf16[512,2048]{1,0:T(8,128)(2,1)}), bf16[2048,2048]{1,0:T(8,128)(2,1)}) %all-gather.20.cloned.1.call-update) | async-done | bytes 8388624 | tf_op jit(solution)/shard_map/all_gather | solution.py:330
  595.4 14.6 fusion.99
  610.0 65.2 %all-gather.26.cloned.1.call-done = bf16[1024,2048]{1,0:T(8,128)(2,1)} async-done(((bf16[256,2048]{1,0:T(8,128)(2,1)}), bf16[1024,2048]{1,0:T(8,128)(2,1)}) %all-gather.26.cloned.1.call-update) | async-done | bytes 4194320 | tf_op jit(solution)/shard_map/all_gather | solution.py:92
  675.2 90.7 %all-gather.24.cloned.1.call-done = bf16[2048,2048]{1,0:T(8,128)(2,1)} async-done(((bf16[2048,512]{1,0:T(8,128)(2,1)}), bf16[2048,2048]{1,0:T(8,128)(2,1)}) %all-gather.24.cloned.1.call-update) | async-done | bytes 8388624 | tf_op jit(solution)/shard_map/all_gather | solution.py:335
  765.9 22.0 %multiply_convert_fusion = (bf16[1024,2048]{1,0:T(8,128)(2,1)}, bf16[1024,2048]{1,0:T(8,128)(2,1)}, bf16[1024,2048]{1,0:T(8,128)(2,1)}) fusion(f32[1024,2048]{1,0:T(8,128)} %fusion.99, f32[1024,2048]{1,0:T(8,128)} %fusion.100, bf16[1024,2048]{1,0:T(8,128)(2,1)} %all-gather.26.cloned.1.call-done, bf16[2048,2048]{1,0:T(8,128)(2,1)} %all-gather.24.cloned.1.call-done), kind=kOutput, calls=%fused_computation.63 | convolution fusion | flops 8621391872 | bytes 41943040 | tf_op jit(solution)/shard_map/td,fd->tf/dot_general | solution.py:393
  787.9 13.1 fusion.101
  801.1 12.9 add_convert_fusion
  814.1 76.9 %reduce-scatter.22.cloned.1.call-done = bf16[256,2048]{1,0:T(8,128)(2,1)} async-done(((bf16[1024,2048]{1,0:T(8,128)(2,1)}), bf16[256,2048]{1,0:T(8,128)(2,1)}) %reduce-scatter.22.cloned.1.call-update) | async-done | bytes 1048592 | tf_op jit(solution)/shard_map/reduce_scatter | solution.py:403
  896.0 78.7 %all-gather.28.cloned.1.call-done = bf16[1024,2048]{1,0:T(8,128)(2,1)} async-done(((bf16[256,2048]{1,0:T(8,128)(2,1)}), bf16[1024,2048]{1,0:T(8,128)(2,1)}) %all-gather.28.cloned.1.call-update) | async-done | bytes 4194320 | tf_op jit(solution)/shard_map/all_gather | solution.py:418
  974.8 6.8 bitcast_reduce_fusion.2
  986.7 91.0 %while.156 = (s32[]{:T(128)}, f32[1024,8,64]{0,2,1:T(8,128)}, f32[1024,8,64]{0,2,1:T(8,128)}, f32[2,512,8,64]{1,0,3,2:T(2,128)}, s32[2]{0:T(128)S(1)}, /*index=5...) while((s32[]{:T(128)}, f32[1024,8,64]{0,2,1:T(8,128)}, ...), condition=%wide.region_27.28_spmd.clone.clone, body=%wide.region_22.27_spmd.clone.clone.sunk | while | flops 1365245952 | bytes 98444472 | solution.py:280
  994.3 17.3 while.159
  996.9 12.2 conditional.6
  1012.7 19.6 %dynamic_update_slice.59 = f32[2,512,8,64]{1,0,3,2:T(2,128)} dynamic-update-slice(f32[2,512,8,64]{1,0,3,2:T(2,128)} %get-tuple-element.3038, f32[1,512,8,64]{1,0,3,2:T(1,128)S(1)} %copy.94, s32[]{:T(128)} %get-tuple-element.3035, s32[]{:T(128)} %constant.395.clone.1..sunk.3, s32[]{:T(128)} %constant.395.clone.1..sunk.3, s32[]{:T(128)} %constant.395.clone.1..sunk.3) | dynamic-update-slice | bytes 2097156 | tf_op jit(solution)/shard_map/while/body/jit(dynamic_update_index_in_dim)/dynamic_update_slice | solution.py:180
  1039.8 17.3 while.159
  1044.9 12.1 conditional.6
  1058.1 19.6 %dynamic_update_slice.59 = f32[2,512,8,64]{1,0,3,2:T(2,128)} dynamic-update-slice(f32[2,512,8,64]{1,0,3,2:T(2,128)} %get-tuple-element.3038, f32[1,512,8,64]{1,0,3,2:T(1,128)S(1)} %copy.94, s32[]{:T(128)} %get-tuple-element.3035, s32[]{:T(128)} %constant.395.clone.1..sunk.3, s32[]{:T(128)} %constant.395.clone.1..sunk.3, s32[]{:T(128)} %constant.395.clone.1..sunk.3) | dynamic-update-slice | bytes 2097156 | tf_op jit(solution)/shard_map/while/body/jit(dynamic_update_index_in_dim)/dynamic_update_slice | solution.py:180
  1077.7 3.1 reshape.325
  1088.4 4.0 fusion.85
  1103.9 14.0 convolution_convert_fusion.2
  1118.1 14.6 convolution_convert_fusion.1
  1132.7 14.1 convolution_convert_fusion
  1146.9 3.2 slice.78
  1150.1 5.8 convolution_convert_fusion.6
  1158.3 41.8 %reduce-scatter.42.cloned.1.call-done = bf16[128,2048]{1,0:T(8,128)(2,1)} async-done(((bf16[512,2048]{1,0:T(8,128)(2,1)}), bf16[128,2048]{1,0:T(8,128)(2,1)}) %reduce-scatter.42.cloned.1.call-update) | async-done | bytes 524304
  1202.3 7.2 convolution_convert_fusion.5
  1209.6 15.0 convolution_convert_fusion.3
  1227.9 48.5 %reduce-scatter.34.cloned.1.call-done = bf16[256,2048]{1,0:T(8,128)(2,1)} async-done(((bf16[2048,2048]{1,0:T(8,128)(2,1)}), bf16[256,2048]{1,0:T(8,128)(2,1)}) %reduce-scatter.34.cloned.1.call-update) | async-done | bytes 1048592 | tf_op jit(solution)/shard_map/reduce_scatter | solution.py:524
  1279.2 72.2 %reduce-scatter.36.cloned.1.call-done = bf16[256,2048]{1,0:T(8,128)(2,1)} async-done(((bf16[2048,2048]{1,0:T(8,128)(2,1)}), bf16[256,2048]{1,0:T(8,128)(2,1)}) %reduce-scatter.36.cloned.1.call-update) | async-done | bytes 1048592 | tf_op jit(solution)/shard_map/reduce_scatter | solution.py:527
  1354.2 71.8 %reduce-scatter.38.cloned.1.call-done = bf16[2048,256]{1,0:T(8,128)(2,1)} async-done(((bf16[2048,2048]{1,0:T(8,128)(2,1)}), bf16[2048,256]{1,0:T(8,128)(2,1)}) %reduce-scatter.38.cloned.1.call-update) | async-done | bytes 1048592 | tf_op jit(solution)/shard_map/reduce_scatter | solution.py:539
  1428.7 42.0 %reduce-scatter.26.cloned.1.call-done = bf16[256,512]{1,0:T(8,128)(2,1)} async-done(((bf16[2048,512]{1,0:T(8,128)(2,1)}), bf16[256,512]{1,0:T(8,128)(2,1)}) %reduce-scatter.26.cloned.1.call-update) | async-done | bytes 262160 | tf_op jit(solution)/shard_map/reduce_scatter | solution.py:512
  1472.5 43.2 %reduce-scatter.32.cloned.1.call-done = bf16[512,256]{1,0:T(8,128)(2,1)} async-done(((bf16[512,2048]{1,0:T(8,128)(2,1)}), bf16[512,256]{1,0:T(8,128)(2,1)}) %reduce-scatter.32.cloned.1.call-update) | async-done | bytes 262160 | tf_op jit(solution)/shard_map/reduce_scatter | solution.py:536
  1517.4 35.8 %reduce-scatter.28.cloned.1.call-done = bf16[256,128]{1,0:T(8,128)(2,1)} async-done(((bf16[2048,128]{1,0:T(8,128)(2,1)}), bf16[256,128]{1,0:T(8,128)(2,1)}) %reduce-scatter.28.cloned.1.call-update) | async-done | bytes 65552 | tf_op jit(solution)/shard_map/reduce_scatter | solution.py:518
  1554.7 35.6 %reduce-scatter.30.cloned.1.call-done = bf16[256,128]{1,0:T(8,128)(2,1)} async-done(((bf16[2048,128]{1,0:T(8,128)(2,1)}), bf16[256,128]{1,0:T(8,128)(2,1)}) %reduce-scatter.30.cloned.1.call-update) | async-done | bytes 65552 | tf_op jit(solution)/shard_map/reduce_scatter | solution.py:521
  1591.8 77.7 %reduce-scatter.24.cloned.1.call-done = bf16[256,2048]{1,0:T(8,128)(2,1)} async-done(((bf16[1024,2048]{1,0:T(8,128)(2,1)}), bf16[256,2048]{1,0:T(8,128)(2,1)}) %reduce-scatter.24.cloned.1.call-update) | async-done | bytes 1048592 | tf_op jit(solution)/shard_map/reduce_scatter | solution.py:456
  1671.7 9.7 all-reduce.5
  1681.6 14.2 all-reduce.4
  1697.0 52.2 %reduce-scatter.20.cloned.1.call-done = bf16[256,2048]{1,0:T(8,128)(2,1)} async-done(((bf16[1024,2048]{1,0:T(8,128)(2,1)}), bf16[256,2048]{1,0:T(8,128)(2,1)}) %reduce-scatter.20.cloned.1.call-update) | async-done | bytes 1048592 | tf_op jit(solution)/shard_map/reduce_scatter | solution.py:384
  1749.2 5.5 fusion.72
  (333 shorter events, 141.5 us)
Async XLA Ops:
  7.2 15.1 copy-start
  7.2 43.7 %all-gather.14.cloned.1.call-start = ((), (), s32[]{:S(2)}) async-start(), calls=%async_computation.14 | async-start | bytes 2621440 | tf_op jit(solution)/shard_map/all_gather | solution.py:327
  7.9 123.3 %all-gather.12.cloned.1.call-start = ((), (), s32[]{:S(2)}) async-start(), calls=%async_computation.13 | async-start | bytes 5242880 | tf_op jit(solution)/shard_map/all_gather | solution.py:92
  16.7 1.6 copy-start.30
  16.7 31.4 %copy-start.41 = (s32[1,8]{1,0:T(1,128)S(1)}, s32[1,8]{1,0:T(1,128)}, u32[]{:S(2)}) copy-start(s32[1,8]{1,0:T(1,128)} %param.29) | copy-start | bytes 100
  21.5 220.1 %all-gather.16.cloned.1.call-start = ((), (), s32[]{:S(2)}) async-start(), calls=%async_computation.15 | async-start | bytes 2621440 | tf_op jit(solution)/shard_map/all_gather | solution.py:334
  22.2 312.2 %reduce-scatter.18.cloned.1.call-start = ((), (), s32[]{:S(2)}) async-start(), calls=%async_computation.16 | async-start | bytes 5242880 | tf_op jit(solution)/shard_map/reduce_scatter | solution.py:366
  49.1 89.4 %copy-start.17 = (f32[1024,64]{0,1:T(8,128)}, f32[1024,64]{0,1:T(8,128)S(1)}, u32[]{:S(2)}) copy-start(f32[1024,64]{0,1:T(8,128)S(1)} %get-tuple-element.2282) | copy-start | bytes 786436
  49.1 89.4 %copy-start.19 = (f32[1024,64]{0,1:T(8,128)}, f32[1024,64]{0,1:T(8,128)S(1)}, u32[]{:S(2)}) copy-start(f32[1024,64]{0,1:T(8,128)S(1)} %get-tuple-element.2281) | copy-start | bytes 786436
  241.5 6.7 copy-start.22
  248.2 86.2 %copy-start.5 = (bf16[256,2048]{1,0:T(8,128)(2,1)S(1)}, bf16[256,2048]{1,0:T(8,128)(2,1)}, u32[]{:S(2)}) copy-start(bf16[256,2048]{1,0:T(8,128)(2,1)} %param.28) | copy-start | bytes 3145732
  248.3 176.1 %all-gather.22.cloned.1.call-start = ((), (), s32[]{:S(2)}) async-start(), calls=%async_computation.19 | async-start | bytes 10485760 | tf_op jit(solution)/shard_map/all_gather | solution.py:331
  248.9 255.8 %all-gather.18.cloned.1.call-start = ((), (), s32[]{:S(2)}) async-start(), calls=%async_computation.17 | async-start | bytes 5242880 | tf_op jit(solution)/shard_map/all_gather | solution.py:92
  265.2 628.6 %copy-start.28 = (f32[4,1,512]{2,1,0:T(1,128)}, f32[4,1,512]{2,1,0:T(1,128)S(1)}, u32[]{:S(2)}) copy-start(f32[4,1,512]{2,1,0:T(1,128)S(1)} %convert_element_type.279) | copy-start | bytes 24580
  336.1 557.8 %copy-start.32 = (f32[256]{0:T(256)}, f32[256]{0:T(256)S(1)}, u32[]{:S(2)}) copy-start(f32[256]{0:T(256)S(1)} %add_rsqrt_fusion) | copy-start | bytes 3076
  338.7 256.8 %all-gather.20.cloned.1.call-start = ((), (), s32[]{:S(2)}) async-start(), calls=%async_computation.18 | async-start | bytes 10485760 | tf_op jit(solution)/shard_map/all_gather | solution.py:330
  339.4 335.8 %all-gather.26.cloned.1.call-start = ((), (), s32[]{:S(2)}) async-start(), calls=%async_computation.22 | async-start | bytes 5242880 | tf_op jit(solution)/shard_map/all_gather | solution.py:92
  340.2 425.7 %all-gather.24.cloned.1.call-start = ((), (), s32[]{:S(2)}) async-start(), calls=%async_computation.20 | async-start | bytes 10485760 | tf_op jit(solution)/shard_map/all_gather | solution.py:335
  340.9 550.0 %reduce-scatter.22.cloned.1.call-start = ((), (), s32[]{:S(2)}) async-start(), calls=%async_computation.23 | async-start | bytes 5242880 | tf_op jit(solution)/shard_map/reduce_scatter | solution.py:403
  787.9 13.2 copy-start.44
  814.0 76.9 %copy-start.8 = (bf16[256,2048]{1,0:T(8,128)(2,1)S(1)}, bf16[256,2048]{1,0:T(8,128)(2,1)}, u32[]{:S(2)}) copy-start(bf16[256,2048]{1,0:T(8,128)(2,1)} %reduce-scatter.18.cloned.1.call-done) | copy-start | bytes 3145732
  814.0 160.7 %all-gather.28.cloned.1.call-start = ((), (), s32[]{:S(2)}) async-start(), calls=%async_computation.24 | async-start | bytes 5242880 | tf_op jit(solution)/shard_map/all_gather | solution.py:418
  890.9 2.9 copy-start.12
  890.9 2.9 copy-start.13
  893.9 2.1 copy-start.37
  896.0 260.1 %reduce-scatter.40.cloned.1.call-start = ((), (), s32[]{:S(2)}) async-start(), calls=%async_computation.33 | async-start | bytes 2621440
  997.3 1.3 copy-start.7
  997.4 1.3 copy-start.11
  998.7 3.0 copy-start.2
  1003.2 2.4 copy-start.14
  1045.4 1.3 copy-start.7
  1045.4 1.3 copy-start.11
  1046.7 3.0 copy-start.2
  1051.2 2.4 copy-start.14
  1077.7 3.1 copy-start.18
  1081.1 1.6 copy-start.10
  1081.3 2.1 copy-start.4
  1083.2 1.6 copy-start.16
  1085.8 2.7 copy-start.40
  1086.3 6.1 copy-start.24
  1086.4 5.9 copy-start.26
  1092.4 1.6 copy-start.21
  1098.9 101.2 %reduce-scatter.42.cloned.1.call-start = ((), (), s32[]{:S(2)}) async-start(), calls=%async_computation.34 | async-start | bytes 2621440
  1103.9 172.5 %reduce-scatter.34.cloned.1.call-start = ((), (), s32[]{:S(2)}) async-start(), calls=%async_computation.30 | async-start | bytes 9437184 | tf_op jit(solution)/shard_map/reduce_scatter | solution.py:524
  1118.0 233.3 %reduce-scatter.36.cloned.1.call-start = ((), (), s32[]{:S(2)}) async-start(), calls=%async_computation.31 | async-start | bytes 9437184 | tf_op jit(solution)/shard_map/reduce_scatter | solution.py:527
  1132.7 293.3 %reduce-scatter.38.cloned.1.call-start = ((), (), s32[]{:S(2)}) async-start(), calls=%async_computation.32 | async-start | bytes 9437184 | tf_op jit(solution)/shard_map/reduce_scatter | solution.py:539
  1146.8 3.3 copy-start.23
  1146.8 323.9 %reduce-scatter.26.cloned.1.call-start = ((), (), s32[]{:S(2)}) async-start(), calls=%async_computation.26 | async-start | bytes 2359296 | tf_op jit(solution)/shard_map/reduce_scatter | solution.py:512
  1150.1 365.6 %reduce-scatter.32.cloned.1.call-start = ((), (), s32[]{:S(2)}) async-start(), calls=%async_computation.29 | async-start | bytes 2359296 | tf_op jit(solution)/shard_map/reduce_scatter | solution.py:536
  1156.0 46.3 %copy-start.25 = (bf16[1024,512]{0,1:T(8,128)(2,1)S(1)}, bf16[1024,512]{0,1:T(8,128)(2,1)}, u32[]{:S(2)}) copy-start(bf16[1024,512]{0,1:T(8,128)(2,1)} %copy-done.24) | copy-start | bytes 3145732
  1156.0 46.3 %copy-start.27 = (bf16[1024,2,64]{0,2,1:T(8,128)(2,1)S(1)}, bf16[1024,2,64]{0,2,1:T(8,128)(2,1)}, u32[]{:S(2)}) copy-start(bf16[1024,2,64]{0,2,1:T(8,128)(2,1)} %copy-done.26) | copy-start | bytes 786436
  1156.0 397.2 %reduce-scatter.28.cloned.1.call-start = ((), (), s32[]{:S(2)}) async-start(), calls=%async_computation.27 | async-start | bytes 589824 | tf_op jit(solution)/shard_map/reduce_scatter | solution.py:518
  1158.3 432.0 %reduce-scatter.30.cloned.1.call-start = ((), (), s32[]{:S(2)}) async-start(), calls=%async_computation.28 | async-start | bytes 589824 | tf_op jit(solution)/shard_map/reduce_scatter | solution.py:521
  1202.2 467.2 %reduce-scatter.24.cloned.1.call-start = ((), (), s32[]{:S(2)}) async-start(), calls=%async_computation.25 | async-start | bytes 5242880 | tf_op jit(solution)/shard_map/reduce_scatter | solution.py:456
  1209.5 539.7 %reduce-scatter.20.cloned.1.call-start = ((), (), s32[]{:S(2)}) async-start(), calls=%async_computation.21 | async-start | bytes 5242880 | tf_op jit(solution)/shard_map/reduce_scatter | solution.py:384
  1224.6 3.1 copy-start.36
  1354.1 315.4 %copy-start.6 = (bf16[256,2048]{1,0:T(8,128)(2,1)S(1)}, bf16[256,2048]{1,0:T(8,128)(2,1)}, u32[]{:S(2)}) copy-start(bf16[256,2048]{1,0:T(8,128)(2,1)} %param.28) | copy-start | bytes 3145732
  1354.1 315.4 %copy-start.31 = (f32[4,1,512]{2,1,0:T(1,128)S(1)}, f32[4,1,512]{2,1,0:T(1,128)}, u32[]{:S(2)}) copy-start(f32[4,1,512]{2,1,0:T(1,128)} %copy-done.30) | copy-start | bytes 24580
  1354.1 315.4 %copy-start.35 = (f32[256]{0:T(256)S(1)}, f32[256]{0:T(256)}, u32[]{:S(2)}) copy-start(f32[256]{0:T(256)} %copy-done.34) | copy-start | bytes 3076
  1354.1 395.1 %copy-start.9 = (bf16[256,2048]{1,0:T(8,128)(2,1)S(1)}, bf16[256,2048]{1,0:T(8,128)(2,1)}, u32[]{:S(2)}) copy-start(bf16[256,2048]{1,0:T(8,128)(2,1)} %reduce-scatter.18.cloned.1.call-done) | copy-start | bytes 3145732
  1354.1 395.1 %copy-start.29 = (f32[4,1,512]{2,1,0:T(1,128)S(1)}, f32[4,1,512]{2,1,0:T(1,128)}, u32[]{:S(2)}) copy-start(f32[4,1,512]{2,1,0:T(1,128)} %copy-done.28) | copy-start | bytes 24580
  1354.2 395.0 %copy-start.33 = (f32[256]{0:T(256)S(1)}, f32[256]{0:T(256)}, u32[]{:S(2)}) copy-start(f32[256]{0:T(256)} %copy-done.32) | copy-start | bytes 3076
  1354.2 395.0 %copy-start.38 = (f32[256]{0:T(256)S(1)}, f32[256]{0:T(256)}, u32[]{:S(2)}) copy-start(f32[256]{0:T(256)} %copy-done.37) | copy-start | bytes 3076
  1697.0 57.7 %copy-start.1 = (bf16[512,512]{1,0:T(8,128)(2,1)S(1)}, bf16[512,512]{1,0:T(8,128)(2,1)}, u32[]{:S(2)}) copy-start(bf16[512,512]{1,0:T(8,128)(2,1)} %param.32) | copy-start | bytes 1572868
  (9 other events, 9.4 us)
Sparse Core Ops, SparseCore 0:
  9.9 40.9 all-gather.13
  53.0 78.1 all-gather.11
  133.0 36.3 all-gather.15
  248.4 85.9 reduce-scatter.17
  336.2 88.1 all-gather.21
  426.5 78.1 all-gather.17
  506.6 88.7 all-gather.19
  597.1 78.1 all-gather.25
  677.2 88.6 all-gather.23
  814.1 76.7 reduce-scatter.21
  896.1 78.6 all-gather.27
  1099.1 54.8 reduce-scatter.39
  1156.9 43.1 reduce-scatter.41
  1203.5 72.8 reduce-scatter.33
  1280.1 71.2 reduce-scatter.35
  1354.7 71.2 reduce-scatter.37
  1429.5 41.1 reduce-scatter.25
  1474.4 41.2 reduce-scatter.31
  1519.0 34.1 reduce-scatter.27
  1556.1 34.1 reduce-scatter.29
  1592.7 76.7 reduce-scatter.23
  1671.8 77.3 reduce-scatter.19
where the time goes:
time: 1770 us; the launch traced here: 1760 us
  waiting for transfers between devices  1220 us (69%)
  matrix products  200 us (11%)
  local copies, waits for them, and re-layouts  161 us (9%)
  blocking collectives  72.8 us (4%)
  other arithmetic  46.7 us (3%)
  loops' own time  41.2 us (2%)
    all_gather x3, waiting for transfers between devices, rows_of_wide(): return lax.all_gather(rows, 'wide', axis=0, tiled=True)  221 us
    all_gather x1, waiting for transfers between devices, on_device(): lax.all_gather(down_weight, 'narrow', axis=1, tiled=True)  90.7 us
    all_gather x1, waiting for transfers between devices, on_device(): lax.all_gather(up_weight, 'narrow', axis=0, tiled=True)  83.4 us
    dynamic_update_slice x8, local copies, waits for them, and re-layouts, attention_forward(): lax.map(query_block, jnp.arange(block_list, dtype=jnp.int32))  82.7 us
    all_gather x1, waiting for transfers between devices, on_device(): hidden_all = lax.all_gather(hidden_low, 'wide', axis=0, tiled=True)  78.7 us
    reduce_scatter x1, waiting for transfers between devices, on_device(): lax.psum_scatter(jnp.einsum('tc,dc->td', projected_low, project_weight, p...  77.7 us
    reduce_scatter x1, waiting for transfers between devices, on_device(): lax.psum_scatter((jnp.einsum('tf,df->td', gate_low, gate_full, preferred_...  76.9 us
    all_gather x1, waiting for transfers between devices, on_device(): lax.all_gather(gate_weight, 'narrow', axis=0, tiled=True)  76.2 us
  transfers between devices with their start and end apart: 22, of which 20 were waited for; matrix products, arithmetic and copies ran while one was open for 13% of the time, Pallas kernels for 0%

commit v1 on v0

v1 whole, which is shorter than its diff:
```python
import functools
import math

import jax
import jax.numpy as jnp
from jax import lax
from jax.experimental import pallas as pl
from jax.experimental.pallas import tpu as pltpu
from jax.sharding import PartitionSpec as P

QUERY_HEADS = 32
KEY_VALUE_HEADS = 8
HEAD_SIZE = 64
LANES = 128

epsilon = 1e-05
masked_score = -1e30
f32 = jnp.float32
bf16 = jnp.bfloat16

ROWS_BY_COLS = (((1,), (0,)), ((), ()))
BOTH_LAST = (((1,), (1,)), ((), ()))
BOTH_FIRST = (((0,), (0,)), ((), ()))
brief = pl.CostEstimate(flops=1024, bytes_accessed=1024, transcendentals=0)


def mm(left, right, dims=ROWS_BY_COLS):
    return lax.dot_general(left, right, dims, preferred_element_type=f32)


def after(value, *earlier):
    return lax.optimization_barrier((value, *earlier))[0]


def fence(*values):
    leaves, tree = jax.tree.flatten(values)
    return jax.tree.unflatten(tree, lax.optimization_barrier(leaves))


def rope_tables(positions, head_dim):
    half_dim = head_dim // 2
    lane = jnp.arange(LANES, dtype=jnp.int32)
    freq_index = (lane % half_dim).astype(f32)
    inverse = 500000.0 ** (-2.0 * freq_index / head_dim)
    wavelength = 2.0 * math.pi / inverse
    smooth_part = (8192.0 / wavelength - 1.0) / 3.0
    blended = (1.0 - smooth_part) * inverse / 32.0 + smooth_part * inverse
    scaled = jnp.where(
        wavelength < 2048.0, inverse, jnp.where(wavelength > 8192.0, inverse / 32.0, blended)
    )
    angles = positions.astype(f32)[:, None] * scaled[None, :]
    sign = jnp.where(lane % head_dim < half_dim, -1.0, 1.0)
    return jnp.cos(angles), jnp.sin(angles) * sign[None, :]


def swap_halves(u, first_half):
    return jnp.where(first_half, pltpu.roll(u, LANES - 32, 1), pltpu.roll(u, 32, 1))


def attention_forward_kernel(
    blocks, pairs, info, proj, cos, sin, start, qs, k2, v2, att, att_low, lse
):
    rows_of = proj.shape[0] // blocks
    own = info[0]
    nq = pairs * LANES
    lane = lax.broadcasted_iota(jnp.int32, (rows_of, LANES), 1)
    low = lane < HEAD_SIZE
    first_half = lane % HEAD_SIZE < HEAD_SIZE // 2

    def prepare(r, carry):
        rows = pl.ds(pl.multiple_of(r * rows_of, rows_of), rows_of)
        c, s = cos[rows, :], sin[rows, :]

        def rotate(u):
            return u * c + swap_halves(u, first_half) * s

        for p in range(pairs):
            u = proj[rows, p * LANES : (p + 1) * LANES]
            qs[rows, p * LANES : (p + 1) * LANES] = (rotate(u) * 0.125).astype(bf16)
        u = proj[rows, nq : nq + LANES]
        turned = pltpu.roll(u, HEAD_SIZE, 1)
        k2[rows, :] = rotate(jnp.where(low, u, turned)).astype(bf16)
        v2[rows, :] = jnp.where(low, turned, u).astype(bf16)
        return carry

    lax.fori_loop(0, blocks, prepare, 0)

    def block(r, carry):
        s = lax.rem(own - r + blocks, blocks)
        rows = pl.ds(pl.multiple_of(r * rows_of, rows_of), rows_of)
        begin = start[rows, :]
        place = s * rows_of + lax.broadcasted_iota(jnp.int32, (rows_of, 1), 0)
        totals = jnp.zeros((rows_of, LANES), f32)
        for p in range(pairs):
            q = qs[rows, p * LANES : (p + 1) * LANES]
            zero = jnp.zeros_like(q)
            halves = (jnp.where(low, q, zero), jnp.where(low, zero, q))

            def step(kb, state, halves=halves):
                kr = lax.rem(own - kb + blocks, blocks)
                krows = pl.ds(pl.multiple_of(kr * rows_of, rows_of), rows_of)
                kc, vc = k2[krows, :], v2[krows, :]
                key = kb * rows_of + lax.broadcasted_iota(jnp.int32, (rows_of, rows_of), 1)
                visible = (key >= begin) & (key <= place)
                new = []
                for qh, (m, l, acc) in zip(halves, state):
                    scores = jnp.where(visible, mm(qh, kc, BOTH_LAST), masked_score)
                    m_new = jnp.maximum(m, jnp.max(scores, -1, keepdims=True))
                    weights = jnp.exp(scores - m_new)
                    scale = jnp.exp(m - m_new)
                    l = scale * l + jnp.sum(weights, -1, keepdims=True)
                    acc = scale * acc + mm(weights.astype(bf16), vc)
                    new.append((m_new, l, acc))
                return tuple(new)

            empty = (
                jnp.full((rows_of, 1), masked_score, f32),
                jnp.zeros((rows_of, 1), f32),
                jnp.zeros((rows_of, LANES), f32),
            )
            (m0, l0, acc0), (m1, l1, acc1) = lax.fori_loop(
                info[1 + s], s + 1, step, (empty, empty)
            )
            out = jnp.where(low, acc0 / l0, acc1 / l1)
            att[rows, p * LANES : (p + 1) * LANES] = out
            att_low[rows, p * LANES : (p + 1) * LANES] = out.astype(bf16)
            totals = jnp.where(lane == 2 * p, m0 + jnp.log(l0), totals)
            totals = jnp.where(lane == 2 * p + 1, m1 + jnp.log(l1), totals)
        lse[rows, :] = totals
        return carry

    lax.fori_loop(0, blocks, block, 0)


def attention_backward_kernel(
    blocks, pairs, info, qs, k2, v2, grad, att, lse, cos, sin, start, *refs
):
    out, dk, dv = refs[-3:]
    rows_of = qs.shape[0] // blocks
    own = info[0]
    nq = pairs * LANES
    lane = lax.broadcasted_iota(jnp.int32, (rows_of, LANES), 1)
    low = lane < HEAD_SIZE
    first_half = lane % HEAD_SIZE < HEAD_SIZE // 2
    dk[...] = jnp.zeros_like(dk)
    dv[...] = jnp.zeros_like(dv)

    def block(r, carry):
        s = lax.rem(own - r + blocks, blocks)
        rows = pl.ds(pl.multiple_of(r * rows_of, rows_of), rows_of)
        begin = start[rows, :]
        place = s * rows_of + lax.broadcasted_iota(jnp.int32, (rows_of, 1), 0)
        totals = lse[rows, :]
        c, sn = cos[rows, :], sin[rows, :]
        for p in range(pairs):
            cols = slice(p * LANES, (p + 1) * LANES)
            q, d = qs[rows, cols], grad[rows, cols]
            zero = jnp.zeros_like(q)
            product = d.astype(f32) * att[rows, cols]
            heads = []
            for h in range(2):
                mine = low if h == 0 else jnp.logical_not(low)
                heads.append(
                    (
                        jnp.where(mine, q, zero),
                        jnp.where(mine, d, zero),
                        jnp.sum(jnp.where(mine, product, 0.0), -1, keepdims=True),
                        jnp.sum(jnp.where(lane == 2 * p + h, totals, 0.0), -1, keepdims=True),
                    )
                )

            def step(kb, state, heads=heads):
                kr = lax.rem(own - kb + blocks, blocks)
                krows = pl.ds(pl.multiple_of(kr * rows_of, rows_of), rows_of)
                kc, vc = k2[krows, :], v2[krows, :]
                key = kb * rows_of + lax.broadcasted_iota(jnp.int32, (rows_of, rows_of), 1)
                visible = (key >= begin) & (key <= place)
                new, dk_add, dv_add = [], None, None
                for (qh, dh, dot, total), dq in zip(heads, state):
                    scores = mm(qh, kc, BOTH_LAST) - total
                    weights = jnp.exp(jnp.where(visible, scores, masked_score))
                    weight_grad = mm(dh, vc, BOTH_LAST)
                    score_low = (weights * (weight_grad - dot)).astype(bf16)
                    new.append(dq + mm(score_low, kc))
                    dk_part = mm(score_low, qh, BOTH_FIRST)
                    dv_part = mm(weights.astype(bf16), dh, BOTH_FIRST)
                    dk_add = dk_part if dk_add is None else dk_add + dk_part
                    dv_add = dv_part if dv_add is None else dv_add + dv_part
                dk[krows, :] += dk_add
                dv[krows, :] += dv_add
                return tuple(new)

            nothing = jnp.zeros((rows_of, LANES), f32)
            dq0, dq1 = lax.fori_loop(info[1 + s], s + 1, step, (nothing, nothing))
            dq = jnp.where(low, dq0, dq1) * 0.125
            out[rows, cols] = (dq * c + swap_halves(dq * sn, first_half)).astype(bf16)
        return carry

    lax.fori_loop(0, blocks, block, 0)

    def finish(r, carry):
        rows = pl.ds(pl.multiple_of(r * rows_of, rows_of), rows_of)

        def total(ref):
            u = ref[rows, :]
            return u + pltpu.roll(u, HEAD_SIZE, 1)

        u = total(dk)
        u = u * cos[rows, :] + swap_halves(u * sin[rows, :], first_half)
        out[rows, nq : nq + LANES] = jnp.where(low, u, total(dv)).astype(bf16)
        return carry

    lax.fori_loop(0, blocks, finish, 0)


def in_vmem(count):
    return [pl.BlockSpec(memory_space=pltpu.VMEM)] * count


def attention_forward(info, proj, cos, sin, start, blocks):
    length = proj.shape[0]
    nq = proj.shape[1] - LANES
    pairs = nq // LANES
    shapes = (
        jax.ShapeDtypeStruct((length, nq), bf16),
        jax.ShapeDtypeStruct((length, LANES), bf16),
        jax.ShapeDtypeStruct((length, LANES), bf16),
        jax.ShapeDtypeStruct((length, nq), f32),
        jax.ShapeDtypeStruct((length, nq), bf16),
        jax.ShapeDtypeStruct((length, LANES), f32),
    )
    return pl.pallas_call(
        functools.partial(attention_forward_kernel, blocks, pairs),
        out_shape=shapes,
        in_specs=[pl.BlockSpec(memory_space=pltpu.SMEM)] + in_vmem(4),
        out_specs=tuple(in_vmem(6)),
        cost_estimate=brief,
        name="attention_forward",
    )(info, proj, cos, sin, start)


def attention_backward(info, splits, saved, grad, cos, sin, start, blocks, kept):
    qs, k2, v2, att, _, lse = saved
    length, nq = qs.shape
    pairs = nq // LANES
    cols = nq + LANES
    args = [info, qs, k2, v2, grad, att, lse, cos, sin, start]
    in_specs = [pl.BlockSpec(x.shape, lambda i, info: (0, 0)) for x in args[1:]]
    aliases = {}
    if kept is not None:
        aliases = {len(args): 0}
        args.append(kept)
        in_specs.append(pl.BlockSpec(memory_space=pl.ANY))
    return pl.pallas_call(
        functools.partial(attention_backward_kernel, blocks, pairs),
        out_shape=jax.ShapeDtypeStruct((length, splits * cols), bf16),
        grid_spec=pltpu.PrefetchScalarGridSpec(
            num_scalar_prefetch=1,
            grid=(1,),
            in_specs=in_specs,
            out_specs=pl.BlockSpec((length, cols), lambda i, info: (0, info[1 + blocks])),
            scratch_shapes=[pltpu.VMEM((length, LANES), f32)] * 2,
        ),
        input_output_aliases=aliases,
        cost_estimate=brief,
        name="attention_backward",
    )(*args)


def absolute_tile(step, core, tiles):
    half = step // tiles
    return (half + core[0] - 2 * half * core[0]) * tiles + step % tiles


def feed_forward_kernel(tiles, core, x, grad, gm, um, dm, go, uo, do, *refs):
    x_all, grad_all, act, gate_up_low, back, out, back_sum, out_sum = refs[-8:]
    tile = act.shape[1]
    i = pl.program_id(0)

    @pl.when(i == 0)
    def _():
        back_sum[...] = jnp.zeros_like(back_sum)
        out_sum[...] = jnp.zeros_like(out_sum)
        x_all[...] = x[...]
        grad_all[...] = grad[...]

    def run(gate_w, up_w, down_w):
        rows = x[...]
        gate_value = mm(rows, gate_w[...])
        up_value = mm(rows, up_w[...])
        act_grad = mm(grad[...], down_w[...], BOTH_LAST)
        sigmoid_gate = jax.nn.sigmoid(gate_value)
        silu_gate = gate_value * sigmoid_gate
        a = (silu_gate * up_value).astype(bf16)
        g = (
            act_grad * up_value * (sigmoid_gate * (1.0 + gate_value * (1.0 - sigmoid_gate)))
        ).astype(bf16)
        u = (act_grad * silu_gate).astype(bf16)
        act[...] = a
        at = pl.multiple_of(absolute_tile(i, core, tiles) * tile, tile)
        gate_up_low[:, pl.ds(at, tile)] = g
        at = pl.multiple_of(at + 2 * tiles * tile, tile)
        gate_up_low[:, pl.ds(at, tile)] = u
        back_sum[...] += mm(g, gate_w[...], BOTH_LAST) + mm(u, up_w[...], BOTH_LAST)
        out_sum[...] += mm(a, down_w[...])

    @pl.when(i < tiles)
    def _():
        run(gm, um, dm)

    @pl.when(i >= tiles)
    def _():
        run(go, uo, do)

    @pl.when(i == 2 * tiles - 1)
    def _():
        back[...] = back_sum[...].astype(bf16)
        out[...] = out_sum[...].astype(bf16)


def feed_forward(part, parts, core, x, grad, own, other, kept):
    rows, width = x.shape
    units = own[1].shape[0]
    tile = min(256, units)
    tiles = units // tile
    first = lambda i: jnp.minimum(i, tiles - 1)
    second = lambda i: jnp.maximum(i - tiles, 0)
    whole = pl.BlockSpec((rows, width), lambda i, c: (0, 0))

    def weights(at):
        return [
            pl.BlockSpec((width, tile), lambda i, c: (0, at(i))),
            pl.BlockSpec((width, tile), lambda i, c: (0, tiles + at(i))),
            pl.BlockSpec((tile, width), lambda i, c: (at(i), 0)),
        ]

    columns = (width, width, 2 * units, 4 * units)
    kept_shapes = tuple(jax.ShapeDtypeStruct((rows * parts, k), bf16) for k in columns)
    kept_specs = (
        pl.BlockSpec((rows, width), lambda i, c: (part, 0)),
        pl.BlockSpec((rows, width), lambda i, c: (part, 0)),
        pl.BlockSpec((rows, tile), lambda i, c: (part, absolute_tile(i, c, tiles))),
        pl.BlockSpec((rows, 4 * units), lambda i, c: (part, 0)),
    )
    args = [core[None], x, grad, own[0], own[0], own[1], other[0], other[0], other[1]]
    in_specs = [whole, whole] + weights(first) + weights(second)
    aliases = {}
    if kept is not None:
        aliases = {len(args) + k: k for k in range(4)}
        args += kept
        in_specs += [pl.BlockSpec(memory_space=pl.ANY)] * 4
    result = pl.pallas_call(
        functools.partial(feed_forward_kernel, tiles),
        out_shape=kept_shapes + (jax.ShapeDtypeStruct((rows, width), bf16),) * 2,
        grid_spec=pltpu.PrefetchScalarGridSpec(
            num_scalar_prefetch=1,
            grid=(2 * tiles,),
            in_specs=in_specs,
            out_specs=kept_specs + (whole,) * 2,
            scratch_shapes=[pltpu.VMEM((rows, width), f32)] * 2,
        ),
        input_output_aliases=aliases,
        cost_estimate=brief,
        name="feed_forward",
    )(*args)
    return list(result[:4]), result[4], result[5]


def on_device(
    tokens,
    document_lengths,
    attn_gain,
    query_projection_weight,
    key_projection_weight,
    value_projection_weight,
    output_weight,
    mlp_gain,
    gate_weight,
    up_weight,
    down_weight,
    output_cotangent,
):
    wide = lax.axis_size("wide")
    narrow = lax.axis_size("narrow")
    cores = lax.axis_size("dp")
    wide_index = lax.axis_index("wide")
    narrow_index = lax.axis_index("narrow")
    core = lax.axis_index("dp")
    other = 1 - core
    local_heads = query_projection_weight.shape[1] // HEAD_SIZE
    group_size = QUERY_HEADS // KEY_VALUE_HEADS
    local_kv = max(1, local_heads // group_size)
    kv_first = wide_index * local_heads // group_size
    nq = local_heads * HEAD_SIZE
    nkv = local_kv * HEAD_SIZE
    own_rows, width = tokens.shape
    length = own_rows * wide
    pairs = local_heads // 2
    half_width = width // 2

    def shift(x, by):
        return lax.ppermute(x, "wide", [(i, (i + by) % wide) for i in range(wide)])

    def swap(x):
        return lax.ppermute(x, "dp", [(i, 1 - i) for i in range(cores)])

    def across(x, bits):
        return lax.ppermute(x, "narrow", [(i, i ^ bits) for i in range(narrow)])

    def ring_reduce(part):
        total = part(1 % wide)
        for k in range(2, wide + 1):
            come = shift(total, 1)
            total = come.astype(f32) + part(k % wide).astype(f32)
            if k < wide:
                total = total.astype(bf16)
        return total

    def narrow_near(x):
        return across(x, 1), across(x, 2)

    def narrow_far(by_x, by_y):
        mid = by_x.shape[0] // 2
        return across(by_x[:mid], 2), across(by_y[mid:], 1)

    def narrow_place(x, near, far, axis):
        rows, cols = x.shape
        size, mid = x.shape[axis], rows // 2
        full = jnp.zeros((rows * narrow, cols) if axis == 0 else (rows, cols * narrow), x.dtype)
        pieces = ((0, x, 0), (1, near[0], 0), (2, near[1], 0), (3, far[0], 0), (3, far[1], mid))
        for bits, piece, row in pieces:
            at = (narrow_index ^ bits) * size
            full = lax.dynamic_update_slice(full, piece, (at + row, 0) if axis == 0 else (row, at))
        return full

    def narrow_scatter(x, axis):
        size = x.shape[axis] // narrow
        cut = x.shape[1 - axis] // 2

        def piece(bits, which):
            begin = [0, 0]
            begin[axis] = (narrow_index ^ bits) * size
            begin[1 - axis] = which * cut
            shape = [cut, cut]
            shape[axis] = size
            return lax.dynamic_slice(x, begin, shape)

        far_b = across(piece(3, 1), 1)
        far_a = across(piece(3, 0), 2)
        x_b = across(piece(1, 1), 1)
        y_a = across(piece(2, 0), 2)
        x_a = across((piece(1, 0).astype(f32) + far_a.astype(f32)).astype(bf16), 1)
        y_b = across((piece(2, 1).astype(f32) + far_b.astype(f32)).astype(bf16), 2)
        first = piece(0, 0).astype(f32) + x_a.astype(f32) + y_a.astype(f32)
        second = piece(0, 1).astype(f32) + x_b.astype(f32) + y_b.astype(f32)
        return first, second

    def sum_all(x):
        x = x + swap(x)
        for axis, size in (("narrow", narrow), ("wide", wide)):
            bits = 1
            while bits < size:
                x = x + lax.ppermute(x, axis, [(i, i ^ bits) for i in range(size)])
                bits *= 2
        return x

    def half(x, which, axis):
        size = x.shape[axis] // 2
        return lax.dynamic_slice_in_dim(x, which * size, size, axis)

    def in_place(x, axis):
        return jnp.where(core == 0, x, exchanged(x, axis))

    def exchanged(x, axis):
        size = x.shape[axis] // 2
        a, b = lax.slice_in_dim(x, 0, size, axis=axis), lax.slice_in_dim(x, size, 2 * size, axis=axis)
        return jnp.concatenate([b, a], axis)

    lengths = document_lengths[0]
    docs = lengths.shape[0]
    upto = jnp.arange(docs)[:, None] <= jnp.arange(docs)[None, :]
    ends = jnp.sum(jnp.where(upto, lengths[:, None], 0), 0)
    starts = ends - lengths

    def start_of(place):
        segment = jnp.sum((place[:, None] >= ends[None, :]).astype(jnp.int32), 1)
        chosen = segment[:, None] == jnp.arange(docs, dtype=jnp.int32)[None, :]
        return jnp.sum(jnp.where(chosen, starts[None, :], 0), 1)

    row = jnp.arange(length, dtype=jnp.int32)
    place = (wide_index - row // own_rows + wide) % wide * own_rows + row % own_rows
    start = start_of(place)
    cos, sin = rope_tables(place - start, HEAD_SIZE)
    columns = start[:, None]
    first_keys = start_of(jnp.arange(wide, dtype=jnp.int32) * own_rows) // own_rows
    info = jnp.concatenate([wide_index[None].astype(jnp.int32), first_keys.astype(jnp.int32)])

    splits = 2 if local_kv % 2 == 0 else 1
    part = own_rows
    nq_half = nq // 2
    token_parts = [tokens, shift(tokens, 1)]
    key_own = lax.dynamic_slice_in_dim(key_projection_weight, kv_first * HEAD_SIZE, nkv, 1)
    value_own = lax.dynamic_slice_in_dim(value_projection_weight, kv_first * HEAD_SIZE, nkv, 1)
    head_weights = (query_projection_weight, key_own, value_own)
    if splits == 2:
        head_weights = tuple(half(x, core, 1) for x in head_weights)
    gains = jnp.stack([attn_gain, mlp_gain], 1)
    gains = jnp.pad(gains, ((0, 0), (0, LANES - 2)))
    head_weights = jnp.concatenate((*head_weights, gains), 1)
    near = narrow_near(head_weights)
    gate_up_half = jnp.concatenate([half(gate_weight, core, 1), half(up_weight, core, 1)], 1)
    gate_up_m = lax.all_gather(gate_up_half, "narrow", axis=0, tiled=True)
    output_half = half(output_weight, core, 0)
    down_half = half(down_weight, core, 0)
    token_parts[1], near, cos, sin, columns, info, output_half, down_half = fence(
        token_parts[1], near, cos, sin, columns, info, output_half, down_half
    )

    token_parts.append(shift(token_parts[1], 1))
    far = narrow_far(*near)
    token_parts[2], far = fence(token_parts[2], far)

    for r in range(3, wide):
        token_parts.append(shift(token_parts[-1], 1))
    ready = after(output_half, token_parts[2])
    wo_parts = [output_half] + [shift(ready, r) for r in range(1, wide)]
    wqkv_m = narrow_place(head_weights, near, far, 0)
    gain_rows = mm(jnp.eye(8, LANES, dtype=bf16), wqkv_m[:, -LANES:], BOTH_LAST)
    wqkv_m = wqkv_m[:, :-LANES]
    wqkv = (wqkv_m, swap(wqkv_m))[:splits]
    attn_gain_row, mlp_gain_row = gain_rows[0:1], gain_rows[1:2]
    normed, invs, projected = [], [], []

    def project(x):
        x = x.astype(f32)
        invs.append(lax.rsqrt(jnp.mean(x * x, -1, keepdims=True) + epsilon))
        normed.append((x * invs[-1] * attn_gain_row).astype(bf16))
        projected.append([mm(normed[-1], w) for w in wqkv])

    def unit(r):
        return token_parts[r].astype(f32) * invs[r]

    for r in range(wide - 2):
        project(token_parts[r])
    token_parts[-1], wo_parts, projected, gate_up_m = fence(
        token_parts[-1], wo_parts, projected, gate_up_m
    )

    def attend(h):
        proj = jnp.concatenate([p[h] for p in projected], 0)
        return attention_forward(info, proj, cos, sin, columns, wide)

    def to_rows(att_low):
        return [att_low[:part]] + [
            shift(att_low[r * part : (r + 1) * part], -r) for r in range(1, wide)
        ]

    grad_parts = [output_cotangent, shift(after(output_cotangent, token_parts[-1]), 1)]
    wo_own = jnp.concatenate([wo_parts[-r % wide] for r in range(wide)], 0)
    wo_m = lax.all_gather(wo_own, "narrow", axis=1, tiled=True)
    down_m = lax.all_gather(after(down_half, wo_own), "narrow", axis=1, tiled=True)
    for r in range(wide - 2, wide):
        project(token_parts[r])
    saved = [attend(0)]
    grad_parts[1], saved, projected = fence(grad_parts[1], saved, projected)

    att_own = [to_rows(saved[0][4])]
    gate_up_o = swap(after(gate_up_m, saved[0][4]))
    if splits == 2:
        saved.append(attend(1))
    att_own, saved, gate_up_o = fence(att_own, saved, gate_up_o)

    if splits == 2:
        att_own.append(to_rows(saved[1][4]))
    else:
        att_own = [[half(a, which, 1) for a in att_own[0]] for which in (core, other)]
    wo_o = swap(after(wo_m, saved[-1][4]))
    att_own = [jnp.concatenate(a, 1) for a in att_own]
    att_own, wo_o = fence(att_own, wo_o)

    grad_parts.append(shift(after(grad_parts[-1], att_own[1]), 1))
    inputs = tokens.astype(f32)
    hidden = inputs + (mm(att_own[0], wo_m) + mm(att_own[1], wo_o))
    inv_second = lax.rsqrt(jnp.mean(hidden * hidden, -1, keepdims=True) + epsilon)
    normed_mlp = (hidden * inv_second * mlp_gain_row).astype(bf16)
    grad_parts[2:], hidden, inv_second, normed_mlp = fence(
        grad_parts[2:], hidden, inv_second, normed_mlp
    )
    unit_second = hidden * inv_second
    down_o = swap(after(down_m, normed_mlp))

    mlp_parts, kept, mlp_outs, first_back, reducing = [normed_mlp], None, [], None, None
    for r in range(wide):
        come = []
        if r + 1 < wide:
            come.append(shift(mlp_parts[r], 1))
        if 3 <= r + 2 < wide:
            come.append(shift(grad_parts[r + 1], 1))
        if r == 2 % wide:
            reducing = shift(back, 1)
        elif r > 2:
            total = reducing.astype(f32) + back.astype(f32)
            reducing = shift(total.astype(bf16), 1)
        kept, back, out = feed_forward(
            r, wide, core, mlp_parts[r], grad_parts[r], (gate_up_m, down_m), (gate_up_o, down_o), kept
        )
        mlp_outs.append(out)
        come, back, reducing = fence(come, back, reducing)
        if r + 1 < wide:
            mlp_parts.append(come[0])
        if 3 <= r + 2 < wide:
            grad_parts.append(come[1])
        if r == 0:
            first_back = back
    mlp_all, grad_all, acts, gate_up_lows = kept

    def rows_sent(left, right):
        return mm(half(left, other, 1), right, BOTH_FIRST).astype(bf16)

    def rows_kept(left, right, come):
        return (mm(half(left, core, 1), right, BOTH_FIRST) + come.astype(f32)).astype(bf16)

    def cols_sent(left, right):
        return mm(left, half(right, other, 1), BOTH_FIRST).astype(bf16)

    def cols_kept(left, right, come):
        return (mm(left, half(right, core, 1), BOTH_FIRST) + come.astype(f32)).astype(bf16)

    def narrow_sum(x, axis):
        return lax.psum_scatter(x, "narrow", scatter_dimension=axis, tiled=True)

    total = reducing.astype(f32) + back.astype(f32)
    reducing = shift(total.astype(bf16), 1)
    down_sent = cols_sent(acts, grad_all)
    gate_up_sent = rows_sent(mlp_all, gate_up_lows)
    reducing, down_sent, gate_up_sent = fence(reducing, down_sent, gate_up_sent)

    normed_mlp_grad = reducing.astype(f32) + first_back.astype(f32)
    out_reducing = shift(after(mlp_outs[1 % wide], reducing), 1)
    down_come, gate_up_come = swap(down_sent), swap(gate_up_sent)
    scaled_second = normed_mlp_grad * mlp_gain_row
    mlp_gain_part = jnp.sum(normed_mlp_grad * unit_second, 0)
    hidden_grad = output_cotangent.astype(f32) + inv_second * (
        scaled_second - unit_second * jnp.mean(scaled_second * unit_second, -1, keepdims=True)
    )
    hidden_low = hidden_grad.astype(bf16)
    head_grads = []
    for w in (wo_m, wo_o):
        back = mm(hidden_low, w, BOTH_LAST).astype(bf16)
        head_grads.append([back[:, r * nq_half : (r + 1) * nq_half] for r in range(wide)])
    if splits == 1:
        head_grads = [[jnp.concatenate(pair, 1) for pair in zip(*head_grads)]]
    out_reducing, down_come, gate_up_come, head_grads, hidden_grad, hidden_low, mlp_gain_part = fence(
        out_reducing, down_come, gate_up_come, head_grads, hidden_grad, hidden_low, mlp_gain_part
    )

    def spread(parts):
        return jnp.concatenate([x if r == 0 else shift(x, r) for r, x in enumerate(parts)], 0)

    def attend_back(h, attended_grad, earlier):
        at = jnp.abs(core - h)[None] * (splits - 1)
        return attention_backward(
            jnp.concatenate([info, at.astype(jnp.int32)]),
            splits, saved[h], attended_grad, cos, sin, columns, wide, earlier,
        )

    attended_grad = spread(head_grads[0])
    if splits == 1:
        attended_grad = in_place(attended_grad, 1)
    down_sum = cols_kept(after(acts, hidden_low), grad_all, down_come)
    att_both = in_place(jnp.concatenate([after(x, hidden_low) for x in att_own], 1), 1)
    out_sent = cols_sent(att_both, hidden_low)
    attended_grad, down_sum, att_both, out_sent = fence(attended_grad, down_sum, att_both, out_sent)

    down_grad = narrow_sum(down_sum, 1).astype(f32)
    out_come = swap(out_sent)
    projected_low = attend_back(0, attended_grad, None)
    if splits == 2:
        attended_grad = spread(head_grads[1])
    attended_grad, projected_low, out_come = fence(attended_grad, projected_low, out_come)

    if wide > 2:
        total = (out_reducing.astype(f32) + mlp_outs[2].astype(f32)).astype(bf16)
        out_reducing = shift(after(total, projected_low), 1)
    if splits == 2:
        projected_low = attend_back(1, attended_grad, projected_low)
    out_sum = cols_kept(att_both, after(hidden_low, attended_grad), out_come)
    wqkv_all = wqkv[0] if splits == 1 else jnp.concatenate(wqkv, 1)
    if splits == 2:
        wqkv_all = in_place(after(wqkv_all, attended_grad), 1)
    out_reducing, projected_low, out_sum, wqkv_all = fence(
        out_reducing, projected_low, out_sum, wqkv_all
    )

    out_sum = narrow_sum(out_sum, 1)
    ng_parts = [
        mm(projected_low[r * part : (r + 1) * part], wqkv_all, BOTH_LAST).astype(bf16) for r in range(wide)
    ]
    normed_grad = shift(ng_parts[1 % wide], 1)
    gate_up_sum = rows_kept(mlp_all, after(gate_up_lows, projected_low), gate_up_come)
    attn_gain_part = sum(jnp.sum(g.astype(f32) * unit(r), 0) for r, g in enumerate(ng_parts))
    normed_grad, ng_parts, gate_up_sum, attn_gain_part = fence(
        normed_grad, ng_parts, gate_up_sum, attn_gain_part
    )

    gate_up_sum = narrow_sum(gate_up_sum, 0)
    normed_all = jnp.concatenate([after(x, normed_grad) for x in normed], 0)
    for k in range(2, wide):
        total = (normed_grad.astype(f32) + ng_parts[k].astype(f32)).astype(bf16)
        normed_grad = shift(total, 1)
        if k == 2:
            project_come = swap(rows_sent(normed_all, projected_low))
            project_sum = rows_kept(normed_all, projected_low, project_come)
            gain_sums = sum_all(jnp.stack([attn_gain_part, mlp_gain_part]))
        if k > 2:
            total = out_reducing.astype(f32) + mlp_outs[k].astype(f32)
            out_reducing = shift(total.astype(bf16), 1)
        if k == 2:
            normed_grad, project_sum, gain_sums = fence(normed_grad, project_sum, gain_sums)
    project_grad = jnp.concatenate(narrow_scatter(project_sum, 0), 1)
    normed_grad = normed_grad.astype(f32) + ng_parts[0].astype(f32)
    mlp_branch = out_reducing.astype(f32) + mlp_outs[0].astype(f32)
    layer_out = (hidden + mlp_branch).astype(bf16)
    scaled_first = normed_grad * attn_gain_row
    tokens_grad = hidden_grad + invs[0] * (
        scaled_first - unit(0) * jnp.mean(scaled_first * unit(0), -1, keepdims=True)
    )

    out_m, out_o = jnp.split(out_sum, 2, 0)

    def out_part(r):
        at = r * nq_half
        return jnp.concatenate([out_m[at : at + nq_half], out_o[at : at + nq_half]], 0)

    output_grad = out_part(0).astype(f32)
    for r in range(1, wide):
        output_grad = output_grad + shift(out_part(r), r).astype(f32)
    gate_grad, up_grad = jnp.split(gate_up_sum.astype(f32), 2, 1)

    heads_grad = jnp.split(project_grad, splits, 1)
    nq_part, nkv_part = nq // splits, nkv // splits
    query_grad = jnp.concatenate([g[:, :nq_part] for g in heads_grad], 1)
    key_grad = jnp.concatenate([g[:, nq_part : nq_part + nkv_part] for g in heads_grad], 1)
    value_grad = jnp.concatenate([g[:, nq_part + nkv_part :] for g in heads_grad], 1)
    total_kv = key_projection_weight.shape[1]

    def kv_grad(part):
        if nkv * wide == total_kv:
            return part
        embed = lax.dynamic_update_slice_in_dim(
            jnp.zeros((part.shape[0], total_kv), bf16), part.astype(bf16), kv_first * HEAD_SIZE, 1
        )
        return lax.psum_scatter(embed, "wide", scatter_dimension=1, tiled=True).astype(f32)

    key_grad, value_grad = kv_grad(key_grad), kv_grad(value_grad)

    gain_own = width // (cores * narrow * wide)
    gain_at = ((core * narrow + narrow_index) * wide + wide_index) * gain_own
    gain_sums = lax.dynamic_slice_in_dim(gain_sums, gain_at, gain_own, 1)
    return (
        layer_out,
        tokens_grad,
        gain_sums[0],
        query_grad,
        key_grad,
        value_grad,
        output_grad,
        gain_sums[1],
        gate_grad,
        up_grad,
        down_grad,
    )


def solution(mesh):
    return jax.shard_map(
        on_device,
        mesh=mesh,
        in_specs=(
            P(("dp", "narrow", "wide"), None),
            P(("dp", "narrow"), None),
            P("narrow"),
            P("narrow", "wide"),
            P("narrow", None),
            P("narrow", None),
            P("wide", "narrow"),
            P("narrow"),
            P("narrow", "wide"),
            P("narrow", "wide"),
            P("wide", "narrow"),
            P(("dp", "narrow", "wide"), None),
        ),
        out_specs=(
            P(("dp", "narrow", "wide"), None),
            P(("dp", "narrow", "wide"), None),
            P(("dp", "narrow", "wide")),
            P(("dp", "narrow"), "wide"),
            P(("dp", "narrow"), "wide"),
            P(("dp", "narrow"), "wide"),
            P("wide", ("dp", "narrow")),
            P(("dp", "narrow", "wide")),
            P(("dp", "narrow"), "wide"),
            P(("dp", "narrow"), "wide"),
            P("wide", ("dp", "narrow")),
        ),
        check_vma=False,
    )
```

time: 1770 us -> 736 us (0.42)
  waiting for transfers between devices: 1220 us -> 234 us
  Pallas kernels: 0 us -> 178 us
  local copies, waits for them, and re-layouts: 161 us -> 50.5 us
  matrix products: 200 us -> 95 us
  starting transfers between devices: 0.89 us -> 85.1 us
  blocking collectives: 72.8 us -> 0 us
  loops' own time: 41.2 us -> 0 us
  other arithmetic: 46.7 us -> 69.5 us
    reduce_scatter x11 -> x3, waiting for transfers between devices: 625 us -> 0.02 us  [narrow_sum(): return lax.psum_scatter(x, 'narrow', scatter_dimension=axis, tiled=True)]
    all_gather x9 -> x3, waiting for transfers between devices: 552 us -> 39.9 us  [the longest x1 26.9 us: on_device(): wo_m = lax.all_gather(wo_own, 'narrow', axis=1, tiled=True)]
    ppermute x0 -> x59, waiting for transfers between devices: none -> 193 us  [the longest x36 125 us: shift(): return lax.ppermute(x, 'wide', [(i, (i + by) % wide) for i in range(wide)])]
    pallas_call x0 -> x8, Pallas kernels: none -> 178 us  [the longest x4 110 us: feed_forward(): pl.pallas_call(functools.partial(feed_forward_kernel, tiles), out_shape=k...]
    dot_general x29 -> x25, matrix products: 200 us -> 95 us  [mm(): return lax.dot_general(left, right, dims, preferred_element_type=f32)]
    ppermute x0 -> x59, starting transfers between devices: none -> 84.8 us  [the longest x36 54.4 us: shift(): return lax.ppermute(x, 'wide', [(i, (i + by) % wide) for i in range(wide)])]
    dynamic_update_slice x10 -> x4, local copies, waits for them, and re-layouts: 87.4 us -> 3.15 us  [narrow_place(): lax.dynamic_update_slice(full, piece, (at + row, 0) if axis == 0 else (ro...]
    all_gather x4 -> x0, blocking collectives: 48.9 us -> none  [the longest x1 16.3 us: on_device(): lax.all_gather(mlp_gain, 'narrow', axis=0, tiled=True)]
  transfers between devices with their start and end apart: 22 -> 65, of which waited for: 20 -> 29; matrix products, arithmetic and copies ran while one was open for 13% -> 25% of each run, Pallas kernels for 0% -> 24%
where the time goes in v1:
time: 736 us; the launch traced here: 727 us
  waiting for transfers between devices  234 us (32%)
  Pallas kernels  178 us (24%)
  matrix products  95 us (13%)
  starting transfers between devices  85.1 us (12%)
  other arithmetic  69.5 us (9%)
  local copies, waits for them, and re-layouts  50.5 us (7%)
  between operations  15.6 us (2%)
    ppermute x36, waiting for transfers between devices, shift(): return lax.ppermute(x, 'wide', [(i, (i + by) % wide) for i in range(wide)])  125 us
    pallas_call x4, Pallas kernels, feed_forward(): pl.pallas_call(functools.partial(feed_forward_kernel, tiles), out_shape=k...  110 us
    dot_general x25, matrix products, mm(): return lax.dot_general(left, right, dims, preferred_element_type=f32)  95 us
    ppermute x36, starting transfers between devices, shift(): return lax.ppermute(x, 'wide', [(i, (i + by) % wide) for i in range(wide)])  54.4 us
    ppermute x10, waiting for transfers between devices, across(): return lax.ppermute(x, 'narrow', [(i, i ^ bits) for i in range(narrow)])  38.4 us
    pallas_call x2, Pallas kernels, attention_backward(): pl.pallas_call(functools.partial(attention_backward_kernel, blocks, pairs...  34.4 us
    pallas_call x2, Pallas kernels, attention_forward(): pl.pallas_call(functools.partial(attention_forward_kernel, blocks, pairs)...  33.1 us
    all_gather x1, waiting for transfers between devices, on_device(): wo_m = lax.all_gather(wo_own, 'narrow', axis=1, tiled=True)  26.9 us
  transfers between devices with their start and end apart: 65, of which 29 were waited for; matrix products, arithmetic and copies ran while one was open for 25% of the time, Pallas kernels for 24%

profile of v1, /device:TPU:8, one launch (start us, length us, event | category | flops | bytes accessed | tf_op | source)
XLA Modules:
  0.0 727.1 jit_solution(17731670964439656362)
XLA Ops:
  21.8 3.1 fusion.41
  24.9 8.6 %collective-permute-done.1 = bf16[512,512]{1,0:T(8,128)(2,1)} collective-permute-done((bf16[512,512]{1,0:T(8,128)(2,1)}, bf16[512,512]{1,0:T(8,128)(2,1)}, u32[]{:S(2)}, u32[]{:S(2)}) %collective-permute-start.1) | collective-permute-done | bytes 524320 | tf_op jit(solution)/shard_map/ppermute | solution.py:408
  35.8 5.9 collective-permute-done
  53.7 3.8 collective-permute-done.4
  57.4 8.6 %collective-permute-done.3 = bf16[256,2048]{1,0:T(8,128)(2,1)} collective-permute-done((bf16[256,2048]{1,0:T(8,128)(2,1)}, bf16[256,2048]{1,0:T(8,128)(2,1)}, u32[]{:S(2)}, u32[]{:S(2)}) %collective-permute-start.3) | collective-permute-done | bytes 1048608 | tf_op jit(solution)/shard_map/ppermute | solution.py:402
  68.7 3.4 collective-permute-start.8
  80.0 2.5 fusion.12
  90.2 17.1 %collective-permute-done.7 = bf16[256,512]{1,0:T(8,128)(2,1)} collective-permute-done((bf16[256,512]{1,0:T(8,128)(2,1)}, bf16[256,512]{1,0:T(8,128)(2,1)}, u32[]{:S(2)}, u32[]{:S(2)}) %collective-permute-start.7) | collective-permute-done | bytes 262176 | tf_op jit(solution)/shard_map/ppermute | solution.py:402
  107.3 2.8 collective-permute-done.8
  110.0 5.3 collective-permute-done.9
  122.6 16.4 %attention_forward.2 = (bf16[1024,256]{1,0:T(8,128)(2,1)}, bf16[1024,128]{1,0:T(8,128)(2,1)}, bf16[1024,128]{1,0:T(8,128)(2,1)}, f32[1024,256]{1,0:T(8,128)}, bf...) custom-call(s32[5]{0:T(128)} %pad_add_fusion.info, f32[1024,384]{1,0:T(8,128)} %pad_maximum_fusion.2.proj, ...), custom_call_target="tpu_custom_call" | custom-call | flops 1024 | bytes 1024 | tf_op jit(solution)/shard_map/attention_forward/pallas_call | solution.py:232
  139.0 2.7 fusion.101
  160.0 16.7 %attention_forward.3 = (bf16[1024,256]{1,0:T(8,128)(2,1)}, bf16[1024,128]{1,0:T(8,128)(2,1)}, bf16[1024,128]{1,0:T(8,128)(2,1)}, f32[1024,256]{1,0:T(8,128)}, bf...) custom-call(s32[5]{0:T(128)} %pad_add_fusion.info, f32[1024,384]{1,0:T(8,128)} %pad_maximum_fusion.3.proj, ...), custom_call_target="tpu_custom_call" | custom-call | flops 1024 | bytes 1024 | tf_op jit(solution)/shard_map/attention_forward/pallas_call | solution.py:232
  176.7 26.9 %all-gather.6.cloned.1.call-done = bf16[1024,2048]{1,0:T(8,128)(2,1)} async-done(((bf16[1024,512]{1,0:T(8,128)(2,1)}), bf16[1024,2048]{1,0:T(8,128)(2,1)}) %all-gather.6.cloned.1.call-update) | async-done | bytes 4194320 | tf_op jit(solution)/shard_map/all_gather | solution.py:560
  211.1 7.0 collective-permute-done.17
  227.1 18.6 %collective-permute-done.20.grad = bf16[256,2048]{1,0:T(8,128)(2,1)} collective-permute-done((bf16[256,2048]{1,0:T(8,128)(2,1)}, bf16[256,2048]{1,0:T(8,128)(2,1)}, u32[]{:S(2)}, u32[]{:S(2)}) %collective-permute-start.20) | collective-permute-done | bytes 1048608 | tf_op jit(solution)/shard_map/ppermute | solution.py:402
  245.7 12.9 %all-gather.8.cloned.1.call-done.dm = bf16[1024,2048]{1,0:T(8,128)(2,1)} async-done(((bf16[1024,512]{1,0:T(8,128)(2,1)}), bf16[1024,2048]{1,0:T(8,128)(2,1)}) %all-gather.8.cloned.1.call-update) | async-done | bytes 4194320 | tf_op jit(solution)/shard_map/all_gather | solution.py:561
  261.7 4.4 collective-permute-done.22.do
  266.1 27.6 %feed_forward.4 = (bf16[1024,2048]{1,0:T(8,128)(2,1)}, bf16[1024,2048]{1,0:T(8,128)(2,1)}, bf16[1024,2048]{1,0:T(8,128)(2,1)}, bf16[1024,4096]{1,0:T(8,128)(2,1)...) custom-call(s32[1]{0:T(128)} %bitcast.8.core, bf16[256,2048]{1,0:T(8,128)(2,1)} %copy-done.30, ...), custom_call_target="tpu_custom_call" | custom-call | flops 1024 | bytes 1024 | tf_op jit(solution)/shard_map/feed_forward/pallas_call | solution.py:352
  295.3 27.6 %feed_forward.5 = (bf16[1024,2048]{1,0:T(8,128)(2,1)}, bf16[1024,2048]{1,0:T(8,128)(2,1)}, bf16[1024,2048]{1,0:T(8,128)(2,1)}, bf16[1024,4096]{1,0:T(8,128)(2,1)...) custom-call(s32[1]{0:T(128)} %bitcast.8.core, ...), custom_call_target="tpu_custom_call", output_to_operand_aliasing={{0}: (9, {}), {1}: (10, {}), {2}: (11, {}), {3}: (12, {})} | custom-call | flops 1024 | bytes 1024 | tf_op jit(solution)/shard_map/feed_forward/pallas_call | solution.py:352
  322.9 6.2 collective-permute-done.23.x
  333.3 27.6 %feed_forward.6 = (bf16[1024,2048]{1,0:T(8,128)(2,1)}, bf16[1024,2048]{1,0:T(8,128)(2,1)}, bf16[1024,2048]{1,0:T(8,128)(2,1)}, bf16[1024,4096]{1,0:T(8,128)(2,1)...) custom-call(s32[1]{0:T(128)} %bitcast.8.core, ...), custom_call_target="tpu_custom_call", output_to_operand_aliasing={{0}: (9, {}), {1}: (10, {}), {2}: (11, {}), {3}: (12, {})} | custom-call | flops 1024 | bytes 1024 | tf_op jit(solution)/shard_map/feed_forward/pallas_call | solution.py:352
  360.9 17.4 %collective-permute-done.26 = bf16[256,2048]{1,0:T(8,128)(2,1)} collective-permute-done((bf16[256,2048]{1,0:T(8,128)(2,1)}, bf16[256,2048]{1,0:T(8,128)(2,1)}, u32[]{:S(2)}, u32[]{:S(2)}) %collective-permute-start.26) | collective-permute-done | bytes 1048608 | tf_op jit(solution)/shard_map/ppermute | solution.py:402
  378.3 2.9 add_convert_fusion.10
  382.1 27.6 %feed_forward.7 = (bf16[1024,2048]{1,0:T(8,128)(2,1)}, bf16[1024,2048]{1,0:T(8,128)(2,1)}, bf16[1024,2048]{1,0:T(8,128)(2,1)}, bf16[1024,4096]{1,0:T(8,128)(2,1)...) custom-call(s32[1]{0:T(128)} %bitcast.8.core, ...), custom_call_target="tpu_custom_call", output_to_operand_aliasing={{0}: (9, {}), {1}: (10, {}), {2}: (11, {}), {3}: (12, {})} | custom-call | flops 1024 | bytes 1024 | tf_op jit(solution)/shard_map/feed_forward/pallas_call | solution.py:352
  413.6 15.0 %convolution_convert_fusion = bf16[1024,4096]{1,0:T(8,128)(2,1)} fusion(bf16[1024,4096]{1,0:T(8,128)(2,1)} %get-tuple-element.309, bf16[1024,2048]{1,0:T(8,128)(2,1)} %get-tuple-element.261, s32[]{:T(128)S(6)} %select_n.204), kind=kOutput, calls=%fused_computation.3 | convolution fusion | flops 8594128896 | bytes 18874372 | tf_op jit(solution)/shard_map/dot_general | solution.py:28
  428.6 6.2 convolution_convert_fusion.2
  439.3 2.8 multiply_reduce_fusion
  442.2 3.6 fusion.86
  450.5 14.2 %collective-permute-done.29 = bf16[256,2048]{1,0:T(8,128)(2,1)} collective-permute-done((bf16[256,2048]{1,0:T(8,128)(2,1)}, bf16[256,2048]{1,0:T(8,128)(2,1)}, u32[]{:S(2)}, u32[]{:S(2)}) %collective-permute-start.29) | collective-permute-done | bytes 1048608 | tf_op jit(solution)/shard_map/ppermute | solution.py:402
  464.7 3.5 collective-permute-start.37
  469.9 8.0 %add_convert_fusion.2 = bf16[2048,1024]{1,0:T(8,128)(2,1)} fusion(bf16[2048,1024]{1,0:T(8,128)(2,1)} %collective-permute-done.30, bf16[1024,2048]{1,0:T(8,128)(2,1)S(1)} %copy-done.6, bf16[1024,2048]{1,0:T(8,128)(2,1)S(1)} %copy-done.4, s32[]{:T(128)S(6)} %select_n.198), kind=kOutput, calls=%fused_computation.2 | convolution fusion | flops 4301258752 | bytes 14680068 | tf_op jit(solution)/shard_map/dot_general | solution.py:28
  479.6 4.3 convolution_convert_fusion.1
  487.1 3.5 pad_maximum_fusion
  491.1 2.9 collective-permute-start.33
  495.0 2.6 add_convert_fusion.8
  497.6 17.2 %attention_backward.2.refs_0_ = bf16[1024,768]{1,0:T(8,128)(2,1)} custom-call(s32[6]{0:T(128)} %get-tuple-element.381.info, bf16[1024,256]{1,0:T(8,128)(2,1)} %get-tuple-element.275.qs, bf16[1024,128]{1,0:T(8,128)(2,1)} %get-tuple-element.276.k2, bf16[1024,128]{1,0:T(8,128)(2,1)} %get-tuple-element.277.v2, bf16[1024,256]{1,0:T(8,128)(2,1)} %pad_maximum_fusion.7.grad, ...), custom_call_target="tpu_custom_call" | custom-call | flops 1024 | bytes 1024 | tf_op jit(solution)/shard_map/attention_backward/pallas_call | solution.py:254
  515.8 17.2 %attention_backward.3 = bf16[1024,768]{1,0:T(8,128)(2,1)} custom-call(s32[6]{0:T(128)} %get-tuple-element.380.info, bf16[1024,256]{1,0:T(8,128)(2,1)} %get-tuple-element.293.qs, bf16[1024,128]{1,0:T(8,128)(2,1)} %get-tuple-element.294.k2, bf16[1024,128]{1,0:T(8,128)(2,1)} %get-tuple-element.295.v2, ...), custom_call_target="tpu_custom_call", output_to_operand_aliasing={{}: (10, {})} | custom-call | flops 1024 | bytes 1024 | tf_op jit(solution)/shard_map/attention_backward/pallas_call | solution.py:254
  533.0 3.4 fusion.88
  536.4 5.5 add_convert_fusion.1
  541.9 4.8 maximum_select_fusion
  548.1 4.3 fusion.15
  554.8 16.1 %add_convert_fusion = bf16[1024,4096]{1,0:T(8,128)(2,1)} fusion(bf16[1024,4096]{1,0:T(8,128)(2,1)} %collective-permute-done.31, bf16[1024,4096]{1,0:T(8,128)(2,1)} %get-tuple-element.309, bf16[1024,2048]{1,0:T(8,128)(2,1)S(1)} %copy-done.2, s32[]{:T(128)S(6)} %select_n.198), kind=kOutput, calls=%fused_computation | convolution fusion | flops 8602517504 | bytes 27262980 | tf_op jit(solution)/shard_map/dot_general | solution.py:28
  570.9 4.1 fusion.20
  575.0 3.4 fusion.13
  578.4 3.3 fusion.11
  582.9 2.7 add_convert_fusion.7
  587.3 3.9 collective-permute-start.44
  593.0 3.4 collective-permute-start.45
  596.4 3.1 fusion.35
  600.6 3.1 collective-permute-done.46
  610.7 2.8 add_convert_fusion.6
  613.5 21.4 %collective-permute-done.48 = f32[2,2048]{1,0:T(2,128)S(1)} collective-permute-done((f32[2,2048]{1,0:T(2,128)S(1)}, f32[2,2048]{1,0:T(2,128)S(1)}, u32[]{:S(2)}, u32[]{:S(2)}) %collective-permute-start.48) | collective-permute-done | bytes 16416 | tf_op jit(solution)/shard_map/ppermute | solution.py:463
  634.9 4.0 add_convert_fusion.3
  639.7 5.7 collective-permute-start.50
  651.0 4.3 collective-permute-done.50
  658.0 4.5 collective-permute-done.52
  662.5 13.5 %collective-permute-done.51 = bf16[256,384]{1,0:T(8,128)(2,1)S(1)} collective-permute-done((bf16[256,384]{1,0:T(8,128)(2,1)S(1)}, bf16[256,384]{1,0:T(8,128)(2,1)S(1)}, u32[]{:S(2)}, u32[]{:S(2)}) %collective-permute-start.51) | collective-permute-done | bytes 196640 | tf_op jit(solution)/shard_map/ppermute | solution.py:408
  678.6 2.7 convert_element_type.337
  693.0 3.0 collective-permute-start.56
  695.9 3.3 fusion.24
  699.2 10.8 %collective-permute-done.57 = bf16[512,256]{1,0:T(8,128)(2,1)S(1)} collective-permute-done((bf16[512,256]{1,0:T(8,128)(2,1)S(1)}, bf16[512,256]{1,0:T(8,128)(2,1)S(1)}, u32[]{:S(2)}, u32[]{:S(2)}) %collective-permute-start.57) | collective-permute-done | bytes 262176 | tf_op jit(solution)/shard_map/ppermute | solution.py:402
  710.0 4.7 collective-permute-done.56
  715.6 4.2 fusion.89
  (366 shorter events, 161.0 us)
Async XLA Ops:
  7.2 108.2 %all-gather.4.cloned.1.call-start = ((), (), s32[]{:S(2)}) async-start(), calls=%async_computation.3 | async-start | bytes 10485760 | tf_op jit(solution)/shard_map/all_gather | solution.py:512
  10.6 193.0 %all-gather.6.cloned.1.call-start = ((), (), s32[]{:S(2)}) async-start(), calls=%async_computation.4 | async-start | bytes 5242880 | tf_op jit(solution)/shard_map/all_gather | solution.py:560
  14.2 19.3 %collective-permute-start.1 = (bf16[512,512]{1,0:T(8,128)(2,1)}, bf16[512,512]{1,0:T(8,128)(2,1)}, u32[]{:S(2)}, u32[]{:S(2)}) collective-permute-start(bf16[512,512]{1,0:T(8,128)(2,1)} %get-tuple-element.332), channel_id=1, source_target_pairs={{0,4},{4,0},{8,12},{12,8},{1,5},{5,1},{9,13},{13,9},{2,6},{6,2},{1... | collective-permute-start | bytes 1572872 | tf_op jit(solution)/shard_map/ppermute | solution.py:408
  15.7 20.2 %collective-permute-start.2 = (bf16[512,512]{1,0:T(8,128)(2,1)}, bf16[512,512]{1,0:T(8,128)(2,1)}, u32[]{:S(2)}, u32[]{:S(2)}) collective-permute-start(bf16[512,512]{1,0:T(8,128)(2,1)} %get-tuple-element.332), channel_id=1, source_target_pairs={{0,8},{4,12},{8,0},{12,4},{1,9},{5,13},{9,1},{13,5},{2,10},{6,14},... | collective-permute-start | bytes 1572872 | tf_op jit(solution)/shard_map/ppermute | solution.py:408
  17.2 24.5 %collective-permute-start = (bf16[256,2048]{1,0:T(8,128)(2,1)S(1)}, bf16[256,2048]{1,0:T(8,128)(2,1)}, u32[]{:S(2)}, u32[]{:S(2)}) collective-permute-start(bf16[256,2048]{1,0:T(8,128)(2,1)S(1)} %copy-done.10), channel_id=1, source_target_pairs={{0,1},{1,2},{2,3},{3,0},{4,5},{5,6},{6,7},{7,4},{8,9},{9,10},{10,1... | collective-permute-start | bytes 3145736 | tf_op jit(solution)/shard_map/ppermute | solution.py:402
  41.7 24.3 %collective-permute-start.3 = (bf16[256,2048]{1,0:T(8,128)(2,1)}, bf16[256,2048]{1,0:T(8,128)(2,1)}, u32[]{:S(2)}, u32[]{:S(2)}) collective-permute-start(bf16[256,2048]{1,0:T(8,128)(2,1)} %collective-permute-done), channel_id=1, source_target_pairs={{0,1},{1,2},{2,3},{3,0},{4,5},{5,6},{6,7},{7,4},{8,9},{9,10},{10,1... | collective-permute-start | bytes 3145736 | tf_op jit(solution)/shard_map/ppermute | solution.py:402
  45.3 12.2 %collective-permute-start.4 = (bf16[256,512]{1,0:T(8,128)(2,1)}, bf16[256,512]{1,0:T(8,128)(2,1)S(1)}, u32[]{:S(2)}, u32[]{:S(2)}) collective-permute-start(bf16[256,512]{1,0:T(8,128)(2,1)} %slice.140), channel_id=1, source_target_pairs={{0,8},{4,12},{8,0},{12,4},{1,9},{5,13},{9,1},{13,5},{2,10},{6,14},... | collective-permute-start | bytes 786440 | tf_op jit(solution)/shard_map/ppermute | solution.py:408
  47.4 10.0 %collective-permute-start.5 = (bf16[256,512]{1,0:T(8,128)(2,1)}, bf16[256,512]{1,0:T(8,128)(2,1)}, u32[]{:S(2)}, u32[]{:S(2)}) collective-permute-start(bf16[256,512]{1,0:T(8,128)(2,1)} %slice.141), channel_id=1, source_target_pairs={{0,4},{4,0},{8,12},{12,8},{1,5},{5,1},{9,13},{13,9},{2,6},{6,2},{1... | collective-permute-start | bytes 786440 | tf_op jit(solution)/shard_map/ppermute | solution.py:408
  66.1 49.3 %collective-permute-start.6 = (bf16[256,2048]{1,0:T(8,128)(2,1)}, bf16[256,2048]{1,0:T(8,128)(2,1)}, u32[]{:S(2)}, u32[]{:S(2)}) collective-permute-start(bf16[256,2048]{1,0:T(8,128)(2,1)} %collective-permute-done.3), channel_id=1, source_target_pairs={{0,1},{1,2},{2,3},{3,0},{4,5},{5,6},{6,7},{7,4},{8,9},{9,10},{10,1... | collective-permute-start | bytes 3145736 | tf_op jit(solution)/shard_map/ppermute | solution.py:402
  67.1 40.1 %collective-permute-start.7 = (bf16[256,512]{1,0:T(8,128)(2,1)}, bf16[256,512]{1,0:T(8,128)(2,1)}, u32[]{:S(2)}, u32[]{:S(2)}) collective-permute-start(bf16[256,512]{1,0:T(8,128)(2,1)} %constant_dynamic-slice_fusion.6), channel_id=1, source_target_pairs={{0,1},{1,2},{2,3},{3,0},{4,5},{5,6},{6,7},{7,4},{8,9},{9,10},{10,1... | collective-permute-start | bytes 786440 | tf_op jit(solution)/shard_map/ppermute | solution.py:402
  68.7 41.4 %collective-permute-start.8 = (bf16[256,512]{1,0:T(8,128)(2,1)}, bf16[256,512]{1,0:T(8,128)(2,1)}, u32[]{:S(2)}, u32[]{:S(2)}) collective-permute-start(bf16[256,512]{1,0:T(8,128)(2,1)} %constant_dynamic-slice_fusion.6), channel_id=1, source_target_pairs={{0,2},{1,3},{2,0},{3,1},{4,6},{5,7},{6,4},{7,5},{8,10},{9,11},{10,... | collective-permute-start | bytes 786440 | tf_op jit(solution)/shard_map/ppermute | solution.py:402
  72.0 43.4 %collective-permute-start.9 = (bf16[256,512]{1,0:T(8,128)(2,1)}, bf16[256,512]{1,0:T(8,128)(2,1)}, u32[]{:S(2)}, u32[]{:S(2)}) collective-permute-start(bf16[256,512]{1,0:T(8,128)(2,1)} %constant_dynamic-slice_fusion.6), channel_id=1, source_target_pairs={{0,3},{1,0},{2,1},{3,2},{4,7},{5,4},{6,5},{7,6},{8,11},{9,8},{10,9... | collective-permute-start | bytes 786440 | tf_op jit(solution)/shard_map/ppermute | solution.py:402
  76.5 10.7 %collective-permute-start.10 = (bf16[2048,384]{1,0:T(8,128)(2,1)S(1)}, bf16[2048,384]{1,0:T(8,128)(2,1)S(1)}, u32[]{:S(2)}, u32[]{:S(2)}) collective-permute-start(bf16[2048,384]{1,0:T(8,128)(2,1)S(1)} %slice.186), channel_id=1, source_target_pairs={{0,16},{16,0},{1,17},{17,1},{2,18},{18,2},{3,19},{19,3},{4,20},{20... | collective-permute-start | bytes 4718600 | tf_op jit(solution)/shard_map/ppermute | solution.py:405
  117.0 25.9 %collective-permute-start.11 = (bf16[256,2048]{1,0:T(8,128)(2,1)}, bf16[256,2048]{1,0:T(8,128)(2,1)}, u32[]{:S(2)}, u32[]{:S(2)}) collective-permute-start(bf16[256,2048]{1,0:T(8,128)(2,1)} %grad.1), channel_id=1, source_target_pairs={{0,1},{1,2},{2,3},{3,0},{4,5},{5,6},{6,7},{7,4},{8,9},{9,10},{10,1... | collective-permute-start | bytes 3145736 | tf_op jit(solution)/shard_map/ppermute | solution.py:402
  143.0 33.7 %collective-permute-start.15 = (bf16[2048,2048]{1,0:T(8,128)(2,1)}, bf16[2048,2048]{1,0:T(8,128)(2,1)}, u32[]{:S(2)}, u32[]{:S(2)}) collective-permute-start(bf16[2048,2048]{1,0:T(8,128)(2,1)} %all-gather.4.cloned.1.call-done.gm.um), channel_id=1, source_target_pairs={{0,16},{16,0},{1,17},{17,1},{2,18},{18,2},{3,19},{19,3},{4,20},{20... | collective-permute-start | bytes 25165832 | tf_op jit(solution)/shard_map/ppermute | solution.py:405
  151.7 107.0 %all-gather.8.cloned.1.call-start = ((), (), s32[]{:S(2)}) async-start(), calls=%async_computation.5 | async-start | bytes 5242880 | tf_op jit(solution)/shard_map/all_gather | solution.py:561
  152.4 526.3 %reduce-scatter.8.cloned.1.call-start = ((), (), s32[]{:S(2)}) async-start(), calls=%async_computation.8 | async-start | bytes 5242880 | tf_op jit(solution)/shard_map/reduce_scatter | solution.py:630
  154.3 22.3 %collective-permute-start.12 = (bf16[256,256]{1,0:T(8,128)(2,1)}, bf16[256,256]{1,0:T(8,128)(2,1)S(1)}, u32[]{:S(2)}, u32[]{:S(2)}) collective-permute-start(bf16[256,256]{1,0:T(8,128)(2,1)} %get-tuple-element.365), channel_id=1, source_target_pairs={{0,3},{1,0},{2,1},{3,2},{4,7},{5,4},{6,5},{7,6},{8,11},{9,8},{10,9... | collective-permute-start | bytes 393224 | tf_op jit(solution)/shard_map/ppermute | solution.py:402
  156.1 20.6 %collective-permute-start.13 = (bf16[256,256]{1,0:T(8,128)(2,1)}, bf16[256,256]{1,0:T(8,128)(2,1)}, u32[]{:S(2)}, u32[]{:S(2)}) collective-permute-start(bf16[256,256]{1,0:T(8,128)(2,1)} %get-tuple-element.364), channel_id=1, source_target_pairs={{0,2},{1,3},{2,0},{3,1},{4,6},{5,7},{6,4},{7,5},{8,10},{9,11},{10,... | collective-permute-start | bytes 393224 | tf_op jit(solution)/shard_map/ppermute | solution.py:402
  156.1 20.6 %collective-permute-start.14 = (bf16[256,256]{1,0:T(8,128)(2,1)}, bf16[256,256]{1,0:T(8,128)(2,1)}, u32[]{:S(2)}, u32[]{:S(2)}) collective-permute-start(bf16[256,256]{1,0:T(8,128)(2,1)} %get-tuple-element.363), channel_id=1, source_target_pairs={{0,1},{1,2},{2,3},{3,0},{4,5},{5,6},{6,7},{7,4},{8,9},{9,10},{10,1... | collective-permute-start | bytes 393224 | tf_op jit(solution)/shard_map/ppermute | solution.py:402
  203.6 16.5 %collective-permute-start.19 = (bf16[1024,2048]{1,0:T(8,128)(2,1)}, bf16[1024,2048]{1,0:T(8,128)(2,1)S(1)}, u32[]{:S(2)}, u32[]{:S(2)}) collective-permute-start(bf16[1024,2048]{1,0:T(8,128)(2,1)} %all-gather.6.cloned.1.call-done), channel_id=1, source_target_pairs={{0,16},{16,0},{1,17},{17,1},{2,18},{18,2},{3,19},{19,3},{4,20},{20... | collective-permute-start | bytes 12582920 | tf_op jit(solution)/shard_map/ppermute | solution.py:405
  204.7 6.3 collective-permute-start.18
  206.3 11.9 %collective-permute-start.17 = (bf16[256,256]{1,0:T(8,128)(2,1)S(1)}, bf16[256,256]{1,0:T(8,128)(2,1)S(1)}, u32[]{:S(2)}, u32[]{:S(2)}) collective-permute-start(bf16[256,256]{1,0:T(8,128)(2,1)S(1)} %get-tuple-element.361), channel_id=1, source_target_pairs={{0,2},{1,3},{2,0},{3,1},{4,6},{5,7},{6,4},{7,5},{8,10},{9,11},{10,... | collective-permute-start | bytes 393224 | tf_op jit(solution)/shard_map/ppermute | solution.py:402
  207.7 12.3 %collective-permute-start.16 = (bf16[256,256]{1,0:T(8,128)(2,1)S(1)}, bf16[256,256]{1,0:T(8,128)(2,1)S(1)}, u32[]{:S(2)}, u32[]{:S(2)}) collective-permute-start(bf16[256,256]{1,0:T(8,128)(2,1)S(1)} %get-tuple-element.362), channel_id=1, source_target_pairs={{0,3},{1,0},{2,1},{3,2},{4,7},{5,4},{6,5},{7,6},{8,11},{9,8},{10,9... | collective-permute-start | bytes 393224 | tf_op jit(solution)/shard_map/ppermute | solution.py:402
  220.1 25.6 %collective-permute-start.20 = (bf16[256,2048]{1,0:T(8,128)(2,1)}, bf16[256,2048]{1,0:T(8,128)(2,1)}, u32[]{:S(2)}, u32[]{:S(2)}) collective-permute-start(bf16[256,2048]{1,0:T(8,128)(2,1)} %collective-permute-done.11.grad), channel_id=1, source_target_pairs={{0,1},{1,2},{2,3},{3,0},{4,5},{5,6},{6,7},{7,4},{8,9},{9,10},{10,1... | collective-permute-start | bytes 3145736 | tf_op jit(solution)/shard_map/ppermute | solution.py:402
  258.6 7.5 %collective-permute-start.22 = (bf16[1024,2048]{1,0:T(8,128)(2,1)}, bf16[1024,2048]{1,0:T(8,128)(2,1)}, u32[]{:S(2)}, u32[]{:S(2)}) collective-permute-start(bf16[1024,2048]{1,0:T(8,128)(2,1)} %all-gather.8.cloned.1.call-done.dm), channel_id=1, source_target_pairs={{0,16},{16,0},{1,17},{17,1},{2,18},{18,2},{3,19},{19,3},{4,20},{20... | collective-permute-start | bytes 12582920 | tf_op jit(solution)/shard_map/ppermute | solution.py:405
  258.6 35.1 %collective-permute-start.21 = (bf16[256,2048]{1,0:T(8,128)(2,1)S(1)}, bf16[256,2048]{1,0:T(8,128)(2,1)}, u32[]{:S(2)}, u32[]{:S(2)}) collective-permute-start(bf16[256,2048]{1,0:T(8,128)(2,1)S(1)} %multiply_convert_fusion.x), channel_id=1, source_target_pairs={{0,1},{1,2},{2,3},{3,0},{4,5},{5,6},{6,7},{7,4},{8,9},{9,10},{10,1... | collective-permute-start | bytes 3145736 | tf_op jit(solution)/shard_map/ppermute | solution.py:402
  260.1 62.8 %collective-permute-start.24 = (bf16[256,2048]{1,0:T(8,128)(2,1)}, bf16[256,2048]{1,0:T(8,128)(2,1)}, u32[]{:S(2)}, u32[]{:S(2)}) collective-permute-start(bf16[256,2048]{1,0:T(8,128)(2,1)} %collective-permute-done.20.grad), channel_id=1, source_target_pairs={{0,1},{1,2},{2,3},{3,0},{4,5},{5,6},{6,7},{7,4},{8,9},{9,10},{10,1... | collective-permute-start | bytes 3145736 | tf_op jit(solution)/shard_map/ppermute | solution.py:402
  293.7 35.4 %collective-permute-start.23 = (bf16[256,2048]{1,0:T(8,128)(2,1)}, bf16[256,2048]{1,0:T(8,128)(2,1)S(1)}, u32[]{:S(2)}, u32[]{:S(2)}) collective-permute-start(bf16[256,2048]{1,0:T(8,128)(2,1)} %collective-permute-done.21.x), channel_id=1, source_target_pairs={{0,1},{1,2},{2,3},{3,0},{4,5},{5,6},{6,7},{7,4},{8,9},{9,10},{10,1... | collective-permute-start | bytes 3145736 | tf_op jit(solution)/shard_map/ppermute | solution.py:402
  330.1 30.8 %collective-permute-start.25 = (bf16[256,2048]{1,0:T(8,128)(2,1)}, bf16[256,2048]{1,0:T(8,128)(2,1)S(1)}, u32[]{:S(2)}, u32[]{:S(2)}) collective-permute-start(bf16[256,2048]{1,0:T(8,128)(2,1)} %copy-done.42), channel_id=1, source_target_pairs={{0,1},{1,2},{2,3},{3,0},{4,5},{5,6},{6,7},{7,4},{8,9},{9,10},{10,1... | collective-permute-start | bytes 3145736 | tf_op jit(solution)/shard_map/ppermute | solution.py:402
  331.6 46.7 %collective-permute-start.26 = (bf16[256,2048]{1,0:T(8,128)(2,1)}, bf16[256,2048]{1,0:T(8,128)(2,1)}, u32[]{:S(2)}, u32[]{:S(2)}) collective-permute-start(bf16[256,2048]{1,0:T(8,128)(2,1)} %get-tuple-element.247), channel_id=1, source_target_pairs={{0,1},{1,2},{2,3},{3,0},{4,5},{5,6},{6,7},{7,4},{8,9},{9,10},{10,1... | collective-permute-start | bytes 3145736 | tf_op jit(solution)/shard_map/ppermute | solution.py:402
  381.2 28.5 %collective-permute-start.27 = (bf16[256,2048]{1,0:T(8,128)(2,1)}, bf16[256,2048]{1,0:T(8,128)(2,1)}, u32[]{:S(2)}, u32[]{:S(2)}) collective-permute-start(bf16[256,2048]{1,0:T(8,128)(2,1)} %add_convert_fusion.10), channel_id=1, source_target_pairs={{0,1},{1,2},{2,3},{3,0},{4,5},{5,6},{6,7},{7,4},{8,9},{9,10},{10,1... | collective-permute-start | bytes 3145736 | tf_op jit(solution)/shard_map/ppermute | solution.py:402
  411.6 25.4 %collective-permute-start.28 = (bf16[256,2048]{1,0:T(8,128)(2,1)S(1)}, bf16[256,2048]{1,0:T(8,128)(2,1)}, u32[]{:S(2)}, u32[]{:S(2)}) collective-permute-start(bf16[256,2048]{1,0:T(8,128)(2,1)S(1)} %add_convert_fusion.9), channel_id=1, source_target_pairs={{0,1},{1,2},{2,3},{3,0},{4,5},{5,6},{6,7},{7,4},{8,9},{9,10},{10,1... | collective-permute-start | bytes 3145736 | tf_op jit(solution)/shard_map/ppermute | solution.py:402
  437.0 27.7 %collective-permute-start.31 = (bf16[1024,4096]{1,0:T(8,128)(2,1)}, bf16[1024,4096]{1,0:T(8,128)(2,1)}, u32[]{:S(2)}, u32[]{:S(2)}) collective-permute-start(bf16[1024,4096]{1,0:T(8,128)(2,1)} %convolution_convert_fusion), channel_id=1, source_target_pairs={{0,16},{16,0},{1,17},{17,1},{2,18},{18,2},{3,19},{19,3},{4,20},{20... | collective-permute-start | bytes 25165832 | tf_op jit(solution)/shard_map/ppermute | solution.py:405
  437.0 27.7 %collective-permute-start.30 = (bf16[2048,1024]{1,0:T(8,128)(2,1)}, bf16[2048,1024]{1,0:T(8,128)(2,1)}, u32[]{:S(2)}, u32[]{:S(2)}) collective-permute-start(bf16[2048,1024]{1,0:T(8,128)(2,1)} %convolution_convert_fusion.2), channel_id=1, source_target_pairs={{0,16},{16,0},{1,17},{17,1},{2,18},{18,2},{3,19},{19,3},{4,20},{20... | collective-permute-start | bytes 12582920 | tf_op jit(solution)/shard_map/ppermute | solution.py:405
  437.5 27.2 %collective-permute-start.29 = (bf16[256,2048]{1,0:T(8,128)(2,1)}, bf16[256,2048]{1,0:T(8,128)(2,1)}, u32[]{:S(2)}, u32[]{:S(2)}) collective-permute-start(bf16[256,2048]{1,0:T(8,128)(2,1)} %get-tuple-element.264), channel_id=1, source_target_pairs={{0,1},{1,2},{2,3},{3,0},{4,5},{5,6},{6,7},{7,4},{8,9},{9,10},{10,1... | collective-permute-start | bytes 3145736 | tf_op jit(solution)/shard_map/ppermute | solution.py:402
  464.7 19.2 %collective-permute-start.37 = (bf16[256,256]{1,0:T(8,128)(2,1)}, bf16[256,256]{1,0:T(8,128)(2,1)}, u32[]{:S(2)}, u32[]{:S(2)}) collective-permute-start(bf16[256,256]{1,0:T(8,128)(2,1)} %get-tuple-element.281), channel_id=1, source_target_pairs={{0,3},{1,0},{2,1},{3,2},{4,7},{5,4},{6,5},{7,6},{8,11},{9,8},{10,9... | collective-permute-start | bytes 393224 | tf_op jit(solution)/shard_map/ppermute | solution.py:402
  468.2 15.7 %collective-permute-start.36 = (bf16[256,256]{1,0:T(8,128)(2,1)}, bf16[256,256]{1,0:T(8,128)(2,1)}, u32[]{:S(2)}, u32[]{:S(2)}) collective-permute-start(bf16[256,256]{1,0:T(8,128)(2,1)} %get-tuple-element.280), channel_id=1, source_target_pairs={{0,2},{1,3},{2,0},{3,1},{4,6},{5,7},{6,4},{7,5},{8,10},{9,11},{10,... | collective-permute-start | bytes 393224 | tf_op jit(solution)/shard_map/ppermute | solution.py:402
  468.2 15.7 %collective-permute-start.35 = (bf16[256,256]{1,0:T(8,128)(2,1)}, bf16[256,256]{1,0:T(8,128)(2,1)}, u32[]{:S(2)}, u32[]{:S(2)}) collective-permute-start(bf16[256,256]{1,0:T(8,128)(2,1)} %get-tuple-element.279), channel_id=1, source_target_pairs={{0,1},{1,2},{2,3},{3,0},{4,5},{5,6},{6,7},{7,4},{8,9},{9,10},{10,1... | collective-permute-start | bytes 393224 | tf_op jit(solution)/shard_map/ppermute | solution.py:402
  485.8 202.3 %reduce-scatter.4.cloned.1.call-start = ((), (), s32[]{:S(2)}) async-start(), calls=%async_computation.6 | async-start | bytes 5242880 | tf_op jit(solution)/shard_map/reduce_scatter | solution.py:630
  485.9 29.8 %collective-permute-start.38 = (bf16[2048,1024]{1,0:T(8,128)(2,1)}, bf16[2048,1024]{1,0:T(8,128)(2,1)}, u32[]{:S(2)}, u32[]{:S(2)}) collective-permute-start(bf16[2048,1024]{1,0:T(8,128)(2,1)} %convolution_convert_fusion.1), channel_id=1, source_target_pairs={{0,16},{16,0},{1,17},{17,1},{2,18},{18,2},{3,19},{19,3},{4,20},{20... | collective-permute-start | bytes 12582920 | tf_op jit(solution)/shard_map/ppermute | solution.py:405
  490.6 24.2 %collective-permute-start.34 = (bf16[256,256]{1,0:T(8,128)(2,1)S(1)}, bf16[256,256]{1,0:T(8,128)(2,1)S(1)}, u32[]{:S(2)}, u32[]{:S(2)}) collective-permute-start(bf16[256,256]{1,0:T(8,128)(2,1)S(1)} %copy-done.58), channel_id=1, source_target_pairs={{0,3},{1,0},{2,1},{3,2},{4,7},{5,4},{6,5},{7,6},{8,11},{9,8},{10,9... | collective-permute-start | bytes 393224 | tf_op jit(solution)/shard_map/ppermute | solution.py:402
  491.1 23.7 %collective-permute-start.33 = (bf16[256,256]{1,0:T(8,128)(2,1)S(1)}, bf16[256,256]{1,0:T(8,128)(2,1)S(1)}, u32[]{:S(2)}, u32[]{:S(2)}) collective-permute-start(bf16[256,256]{1,0:T(8,128)(2,1)S(1)} %copy-done.57), channel_id=1, source_target_pairs={{0,2},{1,3},{2,0},{3,1},{4,6},{5,7},{6,4},{7,5},{8,10},{9,11},{10,... | collective-permute-start | bytes 393224 | tf_op jit(solution)/shard_map/ppermute | solution.py:402
  494.0 20.8 %collective-permute-start.32 = (bf16[256,256]{1,0:T(8,128)(2,1)S(1)}, bf16[256,256]{1,0:T(8,128)(2,1)S(1)}, u32[]{:S(2)}, u32[]{:S(2)}) collective-permute-start(bf16[256,256]{1,0:T(8,128)(2,1)S(1)} %get-tuple-element.272), channel_id=1, source_target_pairs={{0,1},{1,2},{2,3},{3,0},{4,5},{5,6},{6,7},{7,4},{8,9},{9,10},{10,1... | collective-permute-start | bytes 393224 | tf_op jit(solution)/shard_map/ppermute | solution.py:402
  515.7 31.1 %collective-permute-start.39 = (bf16[256,2048]{1,0:T(8,128)(2,1)}, bf16[256,2048]{1,0:T(8,128)(2,1)}, u32[]{:S(2)}, u32[]{:S(2)}) collective-permute-start(bf16[256,2048]{1,0:T(8,128)(2,1)} %add_convert_fusion.8), channel_id=1, source_target_pairs={{0,1},{1,2},{2,3},{3,0},{4,5},{5,6},{6,7},{7,4},{8,9},{9,10},{10,1... | collective-permute-start | bytes 3145736 | tf_op jit(solution)/shard_map/ppermute | solution.py:402
  546.8 168.8 %reduce-scatter.6.cloned.1.call-start = ((), (), s32[]{:S(2)}) async-start(), calls=%async_computation.7 | async-start | bytes 10485760 | tf_op jit(solution)/shard_map/reduce_scatter | solution.py:630
  552.4 29.2 %collective-permute-start.41 = (bf16[256,2048]{1,0:T(8,128)(2,1)}, bf16[256,2048]{1,0:T(8,128)(2,1)}, u32[]{:S(2)}, u32[]{:S(2)}) collective-permute-start(bf16[256,2048]{1,0:T(8,128)(2,1)} %get-tuple-element.391), channel_id=1, source_target_pairs={{0,1},{1,2},{2,3},{3,0},{4,5},{5,6},{6,7},{7,4},{8,9},{9,10},{10,1... | collective-permute-start | bytes 3145736 | tf_op jit(solution)/shard_map/ppermute | solution.py:402
  585.6 25.1 %collective-permute-start.40 = (bf16[256,2048]{1,0:T(8,128)(2,1)}, bf16[256,2048]{1,0:T(8,128)(2,1)}, u32[]{:S(2)}, u32[]{:S(2)}) collective-permute-start(bf16[256,2048]{1,0:T(8,128)(2,1)} %add_convert_fusion.7), channel_id=1, source_target_pairs={{0,1},{1,2},{2,3},{3,0},{4,5},{5,6},{6,7},{7,4},{8,9},{9,10},{10,1... | collective-permute-start | bytes 3145736 | tf_op jit(solution)/shard_map/ppermute | solution.py:402
  587.3 5.7 collective-permute-start.44
  593.0 6.5 collective-permute-start.45
  599.5 35.4 %collective-permute-start.43 = (bf16[1024,768]{1,0:T(8,128)(2,1)}, bf16[1024,768]{1,0:T(8,128)(2,1)}, u32[]{:S(2)}, u32[]{:S(2)}) collective-permute-start(bf16[1024,768]{1,0:T(8,128)(2,1)} %fusion.35), channel_id=1, source_target_pairs={{0,16},{16,0},{1,17},{17,1},{2,18},{18,2},{3,19},{19,3},{4,20},{20... | collective-permute-start | bytes 4718600 | tf_op jit(solution)/shard_map/ppermute | solution.py:405
  603.7 5.1 collective-permute-start.47
  606.1 32.9 %collective-permute-start.42 = (bf16[256,2048]{1,0:T(8,128)(2,1)S(1)}, bf16[256,2048]{1,0:T(8,128)(2,1)S(1)}, u32[]{:S(2)}, u32[]{:S(2)}) collective-permute-start(bf16[256,2048]{1,0:T(8,128)(2,1)S(1)} %add_convert_fusion.5), channel_id=1, source_target_pairs={{0,1},{1,2},{2,3},{3,0},{4,5},{5,6},{6,7},{7,4},{8,9},{9,10},{10,1... | collective-permute-start | bytes 3145736 | tf_op jit(solution)/shard_map/ppermute | solution.py:402
  608.8 26.1 %collective-permute-start.48 = (f32[2,2048]{1,0:T(2,128)S(1)}, f32[2,2048]{1,0:T(2,128)S(1)}, u32[]{:S(2)}, u32[]{:S(2)}) collective-permute-start(f32[2,2048]{1,0:T(2,128)S(1)} %add.367), channel_id=1, source_target_pairs={{0,2},{1,3},{2,0},{3,1},{4,6},{5,7},{6,4},{7,5},{8,10},{9,11},{10,... | collective-permute-start | bytes 49160 | tf_op jit(solution)/shard_map/ppermute | solution.py:463
  639.7 15.6 %collective-permute-start.50 = (bf16[256,384]{1,0:T(8,128)(2,1)S(1)}, bf16[256,384]{1,0:T(8,128)(2,1)S(1)}, u32[]{:S(2)}, u32[]{:S(2)}) collective-permute-start(bf16[256,384]{1,0:T(8,128)(2,1)S(1)} %get-tuple-element.339), channel_id=1, source_target_pairs={{0,8},{4,12},{8,0},{12,4},{1,9},{5,13},{9,1},{13,5},{2,10},{6,14},... | collective-permute-start | bytes 589832 | tf_op jit(solution)/shard_map/ppermute | solution.py:408
  646.8 39.7 %collective-permute-start.49 = (bf16[256,2048]{1,0:T(8,128)(2,1)}, bf16[256,2048]{1,0:T(8,128)(2,1)S(1)}, u32[]{:S(2)}, u32[]{:S(2)}) collective-permute-start(bf16[256,2048]{1,0:T(8,128)(2,1)} %add_convert_fusion.4), channel_id=1, source_target_pairs={{0,1},{1,2},{2,3},{3,0},{4,5},{5,6},{6,7},{7,4},{8,9},{9,10},{10,1... | collective-permute-start | bytes 3145736 | tf_op jit(solution)/shard_map/ppermute | solution.py:402
  647.8 14.7 %collective-permute-start.52 = (bf16[256,384]{1,0:T(8,128)(2,1)S(1)}, bf16[256,384]{1,0:T(8,128)(2,1)S(1)}, u32[]{:S(2)}, u32[]{:S(2)}) collective-permute-start(bf16[256,384]{1,0:T(8,128)(2,1)S(1)} %get-tuple-element.342), channel_id=1, source_target_pairs={{0,8},{4,12},{8,0},{12,4},{1,9},{5,13},{9,1},{13,5},{2,10},{6,14},... | collective-permute-start | bytes 589832 | tf_op jit(solution)/shard_map/ppermute | solution.py:408
  648.9 13.6 %collective-permute-start.54 = (bf16[256,384]{1,0:T(8,128)(2,1)S(1)}, bf16[256,384]{1,0:T(8,128)(2,1)S(1)}, u32[]{:S(2)}, u32[]{:S(2)}) collective-permute-start(bf16[256,384]{1,0:T(8,128)(2,1)S(1)} %get-tuple-element.340), channel_id=1, source_target_pairs={{0,4},{4,0},{8,12},{12,8},{1,5},{5,1},{9,13},{13,9},{2,6},{6,2},{1... | collective-permute-start | bytes 589832 | tf_op jit(solution)/shard_map/ppermute | solution.py:408
  649.8 31.6 %collective-permute-start.53 = (bf16[256,384]{1,0:T(8,128)(2,1)}, bf16[256,384]{1,0:T(8,128)(2,1)}, u32[]{:S(2)}, u32[]{:S(2)}) collective-permute-start(bf16[256,384]{1,0:T(8,128)(2,1)} %get-tuple-element.341), channel_id=1, source_target_pairs={{0,4},{4,0},{8,12},{12,8},{1,5},{5,1},{9,13},{13,9},{2,6},{6,2},{1... | collective-permute-start | bytes 589832 | tf_op jit(solution)/shard_map/ppermute | solution.py:408
  655.4 20.5 %collective-permute-start.51 = (bf16[256,384]{1,0:T(8,128)(2,1)S(1)}, bf16[256,384]{1,0:T(8,128)(2,1)S(1)}, u32[]{:S(2)}, u32[]{:S(2)}) collective-permute-start(bf16[256,384]{1,0:T(8,128)(2,1)S(1)} %add_convert_fusion.12), channel_id=1, source_target_pairs={{0,4},{4,0},{8,12},{12,8},{1,5},{5,1},{9,13},{13,9},{2,6},{6,2},{1... | collective-permute-start | bytes 589832 | tf_op jit(solution)/shard_map/ppermute | solution.py:408
  676.7 6.0 collective-permute-start.55
  689.8 9.4 %collective-permute-start.58 = (bf16[512,256]{1,0:T(8,128)(2,1)S(1)}, bf16[512,256]{1,0:T(8,128)(2,1)S(1)}, u32[]{:S(2)}, u32[]{:S(2)}) collective-permute-start(bf16[512,256]{1,0:T(8,128)(2,1)S(1)} %pad_maximum_fusion.11), channel_id=1, source_target_pairs={{0,3},{1,0},{2,1},{3,2},{4,7},{5,4},{6,5},{7,6},{8,11},{9,8},{10,9... | collective-permute-start | bytes 786440 | tf_op jit(solution)/shard_map/ppermute | solution.py:402
  690.9 19.1 %collective-permute-start.57 = (bf16[512,256]{1,0:T(8,128)(2,1)S(1)}, bf16[512,256]{1,0:T(8,128)(2,1)S(1)}, u32[]{:S(2)}, u32[]{:S(2)}) collective-permute-start(bf16[512,256]{1,0:T(8,128)(2,1)S(1)} %pad_maximum_fusion.10), channel_id=1, source_target_pairs={{0,2},{1,3},{2,0},{3,1},{4,6},{5,7},{6,4},{7,5},{8,10},{9,11},{10,... | collective-permute-start | bytes 786440 | tf_op jit(solution)/shard_map/ppermute | solution.py:402
  693.0 21.7 %collective-permute-start.56 = (bf16[512,256]{1,0:T(8,128)(2,1)S(1)}, bf16[512,256]{1,0:T(8,128)(2,1)S(1)}, u32[]{:S(2)}, u32[]{:S(2)}) collective-permute-start(bf16[512,256]{1,0:T(8,128)(2,1)S(1)} %pad_maximum_fusion.9), channel_id=1, source_target_pairs={{0,1},{1,2},{2,3},{3,0},{4,5},{5,6},{6,7},{7,4},{8,9},{9,10},{10,1... | collective-permute-start | bytes 786440 | tf_op jit(solution)/shard_map/ppermute | solution.py:402
  (77 other events, 699.1 us)
Sparse Core Ops, SparseCore 0:
  10.8 99.9 all-gather.3
  151.8 51.7 all-gather.5
  206.0 52.5 all-gather.7
  485.9 52.2 reduce-scatter.7
  546.9 59.9 reduce-scatter.3
  609.8 98.4 reduce-scatter.5
